TPU v7x, 32 devices: a whole 2x2x4 slice. The times are simulated.
32 devices in a mesh: groups: 2 (over y), ctx: 4 (over z), head: 2 (over x), sub: 2 (over core).
Axes of the slice: x: 2, y: 2, z: 4, core: 2. Of those that a mesh axis runs over, the one named last changes fastest.
Arguments:
- queries: float32 [1024, 32, 128], P(('groups', 'ctx'), ('head', 'sub')), parts along dimension 0, may hold values from -110 to 110
- key_vectors: float32 [1024, 8, 128], P(('groups', 'ctx'), 'head'), parts along dimension 0, may hold values from -110 to 110
- value_vectors: float32 [1024, 8, 128], P(('groups', 'ctx'), 'head'), parts along dimension 0, may hold values from -20 to 20
- query_feature: float32 [32, 128, 128], P(('head', 'sub')), may hold values from -0.5 to 0.5
- key_feature: float32 [32, 128, 128], P(('head', 'sub')), may hold values from -0.5 to 0.5
Outputs:
- query_grad: float32 [1024, 32, 128], P(('groups', 'ctx'), ('head', 'sub')), parts along dimension 0
- key_grad: float32 [1024, 8, 128], P(('groups', 'ctx'), 'head'), parts along dimension 0
- value_grad: float32 [1024, 8, 128], P(('groups', 'ctx'), 'head'), parts along dimension 0
There are 2 independent parts, one for each index of `groups`. A program takes and returns all parts, laid end to end along the dimension named above; an argument that names none is the same for every part. Nothing has to cross between parts.
All inputs are finite; a program needn't handle non-finite values.
Results may differ from a plain program's by a relative error of at most 0.0003.
Values sent between devices are 32-bit elements; how exact they have to be, the bound alone decides.
No kernel may reach another device: no remote copies, remote signals or barrier semaphores. Data moves between devices by JAX's collectives and lax.ppermute only.
A program may use at most 64 MiB of HBM per device.

v0:
```python
import functools
import math

import jax
import jax.numpy as jnp
from jax import lax
from jax.experimental import pallas as pl
from jax.experimental.pallas import tpu as pltpu
from jax.sharding import PartitionSpec as P


NEG = -1e30
F32 = jnp.float32
BF16 = jnp.bfloat16

NT = (((1,), (1,)), ((), ()))
NN = (((1,), (0,)), ((), ()))


def shifted(value, axis, steps):
    count = lax.axis_size(axis)
    first, last = max(0, -steps), min(count, count - steps)
    return lax.ppermute(value, axis, [(i, i + steps) for i in range(first, last)])


def split2(x):
    hi = x.astype(BF16)
    return hi, (x - hi.astype(F32)).astype(BF16)


def split3(x):
    hi = x.astype(BF16)
    rest = x - hi.astype(F32)
    mid = rest.astype(BF16)
    return hi, mid, (rest - mid.astype(F32)).astype(BF16)


def lanes(*parts):
    return jnp.concatenate(parts, axis=1)


def stack(*parts):
    return jnp.concatenate(parts, axis=0)


def dot(a, b, dims):
    return lax.dot_general(a, b, dims, preferred_element_type=F32)


def short3(a, b, dims):
    join = lanes if dims is NT else stack
    return dot(lanes(a[0], a[0], a[1]), join(b[0], b[1], b[0]), dims)


def short6(a, b, dims):
    join = lanes if dims is NT else stack
    return dot(
        lanes(a[1], a[2], a[0], a[1], a[0], a[0]),
        join(b[1], b[0], b[2], b[0], b[1], b[0]),
        dims,
    )


def tall3(a, b, dims):
    m = a[0].shape[0]
    both = dot(stack(a[0], a[1]), b[0], dims)
    return both[:m] + (both[m:] + dot(a[0], b[1], dims))


def wide3(a, b, dims):
    if dims is NT:
        n = b[0].shape[0]
        both = dot(a[0], stack(b[0], b[1]), dims)
    else:
        n = b[0].shape[1]
        both = dot(a[0], lanes(b[0], b[1]), dims)
    return both[:, :n] + (both[:, n:] + dot(a[1], b[0], dims))


def colsum(x):
    return jnp.sum(x, axis=0, keepdims=True)


def colmax(x):
    return jnp.max(x, axis=0, keepdims=True)


def softmax_pair(mapped):
    up = jnp.exp(mapped - colmax(mapped))
    low = jnp.exp(jnp.min(mapped, axis=0, keepdims=True) - mapped)
    return stack(up * (1.0 / colsum(up)), low * (1.0 / colsum(low)))


def softmax_pair_back(feat, grad, width):
    up, low = feat[:width], feat[width:]
    gup, glow = grad[:width], grad[width:]
    return up * (gup - colsum(up * gup)) - low * (glow - colsum(low * glow))


def pack_kernel(cfg, k_hbm, v_hbm, *refs):
    kv_refs, (k_ref, v_ref, sems) = refs[: cfg.groups], refs[cfg.groups :]
    copies = [
        pltpu.make_async_copy(src, dst, sems.at[i])
        for i, (src, dst) in enumerate(((k_hbm, k_ref), (v_hbm, v_ref)))
    ]
    for copy in copies:
        copy.start()
    sub = lax.axis_index("sub")
    for slot, ref in enumerate((k_ref, v_ref)):
        copies[slot].wait()
        for g, kv_ref in enumerate(kv_refs):
            value = ref[:, cfg.starts[0] + g, :]
            for s in range(1, len(cfg.starts)):
                value = jnp.where(sub == s, ref[:, cfg.starts[s] + g, :], value)
            kv_ref[slot] = value


def prep_kernel(cfg, q_ref, wq_ref, wk_ref, *refs):
    own_refs, outs = refs[: cfg.groups], refs[cfg.groups :]
    tokens, width, per_group = cfg.tokens, cfg.width, cfg.per_group
    rows = per_group * tokens
    scale = 1.0 / math.sqrt(width)
    key_row = lax.broadcasted_iota(jnp.int32, (tokens, rows), 0)
    query_col = lax.broadcasted_iota(jnp.int32, (tokens, rows), 1) % tokens
    for g in range(cfg.groups):
        (
            q_out, wk_out, fq_out, wk2_out, wq2_out, a_out, num_out, top_out, mass_out
        ) = outs[g::cfg.groups]
        first = g * per_group
        query = split3(stack(*[q_ref[:, first + h, :] for h in range(per_group)]))
        for i in range(3):
            q_out[:, i * width : (i + 1) * width] = query[i]
        scores = short6(split3(own_refs[g][0]), query, NT) * scale
        scores = jnp.where(key_row <= query_col, scores, NEG)
        top = colmax(scores)
        a = jnp.exp(scores - top)
        a_out[...] = a
        top_out[...] = top
        mass_out[...] = colsum(a)
        num_out[...] = short3(split2(own_refs[g][1].T), split2(a), NN)
        for h in range(per_group):
            piece = tuple(x[h * tokens : (h + 1) * tokens] for x in query)
            feat = split2(softmax_pair(short6(split3(wq_ref[first + h].T), piece, NT)))
            fq_out[h, :, :tokens] = feat[0]
            fq_out[h, :, tokens:] = feat[1]
            part = split3(wk_ref[first + h].T)
            for i in range(3):
                wk_out[h * width : (h + 1) * width, i * width : (i + 1) * width] = part[i]
            for out, part in (
                (wk2_out, split2(wk_ref[first + h])),
                (wq2_out, split2(wq_ref[first + h])),
            ):
                for i in range(2):
                    at = i * per_group + h
                    out[:, at * width : (at + 1) * width] = part[i]


def attend_kernel(cfg, *refs):
    n = cfg.devices
    q_ref, wk_t_ref, fq_ref, wk2_ref, a_ref, num_ref, top_ref, mass_ref = refs[:8]
    kv_in = (None,) + refs[8 : 7 + n]
    win_ref, grad_ref, gden_ref, dfq_s = refs[7 + n : 11 + n]
    kv_out = (None, None) + refs[11 + n : 9 + 2 * n]
    (kv_s, dkv_s, top_s, mass_s, tnum_s, num_s, den_s, c_s, fk_s) = refs[9 + 2 * n :]
    here = lax.axis_index("ctx")
    tokens, width, per_group = cfg.tokens, cfg.width, cfg.per_group
    scale = 1.0 / math.sqrt(width)

    for k in range(2, n):
        pair, at = k // 2 - 1, (k % 2) * tokens
        for slot in range(2):
            kv_s[pair, slot, at : at + tokens, :] = kv_in[k][slot]
    query = tuple(q_ref[:, i * width : (i + 1) * width] for i in range(3))

    def head(x, h):
        return x[:, h * tokens : (h + 1) * tokens]

    def fq(h):
        return fq_ref[h, :, :tokens], fq_ref[h, :, tokens:]

    key_prev, value_prev = kv_in[1][0], kv_in[1][1]
    s_prev = short6(split3(key_prev), query, NT) * scale
    s_prev = jnp.where(here > 0, s_prev, NEG)
    top = jnp.maximum(top_ref[...], colmax(s_prev))
    a_prev = jnp.exp(s_prev - top)
    fade = jnp.exp(top_ref[...] - top)
    a_own = a_ref[...] * fade
    win_ref[:tokens] = a_own
    win_ref[tokens:] = a_prev
    mass = mass_ref[...] * fade + colsum(a_prev)
    wnum = num_ref[...] * fade + short3(
        split2(value_prev.T), split2(a_prev), NN
    )
    top_s[...] = top
    mass_s[...] = mass
    tnum_s[...] = wnum
    num_s[...] = wnum
    den_s[...] = mass

    def far_forward(pair, carry):
        second = here >= 2 * pair + 3
        key, value = kv_s[pair, 0], kv_s[pair, 1]
        key_3 = split3(key)
        s = short6(key_3, query, NT) * scale
        s = stack(s[:tokens], jnp.where(second, s[tokens:], NEG))
        old = top_s[...]
        new = jnp.maximum(old, colmax(s))
        p = jnp.exp(s - new)
        factor = jnp.exp(old - new)
        top_s[...] = new
        mass_s[...] = mass_s[...] * factor + colsum(p)
        wk_t = tuple(wk_t_ref[:, i * width : (i + 1) * width] for i in range(3))
        mapped = short6(wk_t, key_3, NT)
        for h in range(per_group):
            feat_t = softmax_pair(mapped[h * width : (h + 1) * width])
            fk_s[pair, h] = feat_t
            c = wide3(split2(feat_t.T), fq(h), NN)
            c_s[pair, :tokens, h * tokens : (h + 1) * tokens] = c[:tokens]
            c_s[pair, tokens:, h * tokens : (h + 1) * tokens] = jnp.where(
                second, c[tokens:], 0.0
            )
        c = c_s[pair]
        den_s[...] += colsum(c)
        value_t = split2(value.T)
        tnum_s[...] = tnum_s[...] * factor + tall3(value_t, split2(p), NN)
        num_s[...] += tall3(value_t, split2(c), NN)
        return carry

    pairs = here // 2
    lax.fori_loop(0, pairs, far_forward, 0)

    inv = 1.0 / den_s[...]
    out = num_s[...] * inv
    residual = out - tnum_s[...] * (1.0 / mass_s[...])
    grad = residual * inv
    grad_2 = split2(grad)
    grad_ref[0] = grad_2[0]
    grad_ref[1] = grad_2[1]
    grad_den = -colsum(residual * out) * inv
    gden_ref[...] = grad_den
    dfq_s[...] = jnp.zeros_like(dfq_s)

    def far_backward(pair, carry):
        second = here >= 2 * pair + 3
        dc = short3(split2(kv_s[pair, 1]), grad_2, NN) + grad_den
        dc = stack(dc[:tokens], jnp.where(second, dc[tokens:], 0.0))
        dc_2 = split2(dc)
        dkv_s[pair, 1] = wide3(split2(c_s[pair]), grad_2, NT)
        pieces = []
        for h in range(per_group):
            feat_t = fk_s[pair, h]
            dc_h = tuple(head(x, h) for x in dc_2)
            dfq_s[h] += wide3(split2(feat_t), dc_h, NN)
            dfk = short3(fq(h), dc_h, NT)
            pieces.append(softmax_pair_back(feat_t, dfk, width))
        wk_2 = wk2_ref[:, : per_group * width], wk2_ref[:, per_group * width :]
        dkv_s[pair, 0] = tall3(wk_2, split2(stack(*pieces)), NN).T
        return carry

    lax.fori_loop(0, pairs, far_backward, 0)
    for k in range(2, n):
        pair, at = k // 2 - 1, (k % 2) * tokens

        @pl.when(here >= k)
        def _():
            for slot in range(2):
                kv_out[k][slot] = dkv_s[pair, slot, at : at + tokens, :]

        @pl.when(here < k)
        def _():
            kv_out[k][...] = jnp.zeros((2, tokens, width), F32)


def window_kernel(cfg, *refs):
    q_ref, win_ref, grad_ref, gden_ref, own_ref, prev_ref, soft_ref = refs[:7]
    outs = refs[7:]
    tokens, width = cfg.tokens, cfg.width
    scale = 1.0 / math.sqrt(width)
    grad_2 = grad_ref[0], grad_ref[1]
    win = win_ref[...]
    soft = short3(split2(stack(own_ref[1], prev_ref[1])), grad_2, NN) + gden_ref[...]
    soft_2 = split2(win * soft * scale)
    soft_ref[0] = soft_2[0]
    soft_ref[1] = soft_2[1]
    dk = wide3(soft_2, (q_ref[:, :width], q_ref[:, width : 2 * width]), NN)
    dv = wide3(split2(win), grad_2, NT)
    for k, out in enumerate(outs):
        out[0] = dk[k * tokens : (k + 1) * tokens]
        out[1] = dv[k * tokens : (k + 1) * tokens]


def query_kernel(cfg, *refs):
    dq_ref = refs[-1]
    tokens, width, per_group = cfg.tokens, cfg.width, cfg.per_group
    for g in range(cfg.groups):
        soft_ref, dfq_ref, fq_ref, wq2_ref, own_ref, prev_ref = refs[:-1][g :: cfg.groups]
        key_t = split2(stack(own_ref[0], prev_ref[0]).T)
        dq = tall3(key_t, (soft_ref[0], soft_ref[1]), NN)
        for h in range(per_group):
            feat = fq_ref[h, :, :tokens].astype(F32) + fq_ref[h, :, tokens:].astype(F32)
            back = softmax_pair_back(feat, dfq_ref[h], width)
            wq_2 = tuple(
                wq2_ref[:, (i * per_group + h) * width : (i * per_group + h + 1) * width]
                for i in range(2)
            )
            dq_h = dq[:, h * tokens : (h + 1) * tokens] + short3(wq_2, split2(back), NN)
            dq_ref[:, g * per_group + h, :] = dq_h.T


def add_kernel(*refs):
    total = refs[0][...]
    for ref in refs[1:-1]:
        total = total + ref[...]
    refs[-1][...] = total


def place_kernel(cfg, *refs):
    sub = lax.axis_index("sub")
    mine, other = refs[: cfg.groups], refs[cfg.groups : 2 * cfg.groups]
    for slot, ref in enumerate(refs[2 * cfg.groups :]):
        for g in range(cfg.groups_dev):
            if cfg.shared:
                ref[:, g, :] = mine[g][slot] + other[g][slot]
            else:
                owner, at = g // cfg.groups, g % cfg.groups
                ref[:, g, :] = jnp.where(sub == owner, mine[at][slot], other[at][slot])


class Config:
    def __init__(self, queries, key_vectors):
        self.tokens, self.heads, self.width = queries.shape
        self.groups_dev = key_vectors.shape[1]
        self.devices = lax.axis_size("ctx")
        subs = lax.axis_size("sub")
        assert subs == 2
        size = self.heads * subs // self.groups_dev
        self.shared = self.heads < size
        self.groups = max(1, self.heads // size)
        self.per_group = self.heads // self.groups
        self.starts = [s * self.heads // size for s in range(subs)]
        if self.shared:
            assert self.groups_dev == 1


VMEM = pl.BlockSpec(memory_space=pltpu.VMEM)


def limit(mebibytes):
    return pltpu.CompilerParams(vmem_limit_bytes=mebibytes << 20)


def near(*arrays):
    return [pltpu.with_memory_space_constraint(x, pltpu.VMEM) for x in arrays]


def call(kernel, outs, args, scratch=(), ins=None, megabytes=16):
    return pl.pallas_call(
        kernel,
        out_shape=outs,
        in_specs=ins or [VMEM] * len(args),
        out_specs=jax.tree.map(lambda _: VMEM, outs),
        scratch_shapes=scratch,
        compiler_params=limit(megabytes),
    )(*args)


def layer(queries, key_vectors, value_vectors, query_feature, key_feature):
    cfg = Config(queries, key_vectors)
    tokens, width, groups, per_group = cfg.tokens, cfg.width, cfg.groups, cfg.per_group
    n, rows = cfg.devices, cfg.per_group * cfg.tokens
    pairs = max(1, (n - 1) // 2)
    kv_shape = pltpu.VMEM((2, tokens, width), F32)
    own = call(
        functools.partial(pack_kernel, cfg),
        (kv_shape,) * groups,
        (key_vectors, value_vectors),
        [
            pltpu.VMEM(key_vectors.shape, F32),
            pltpu.VMEM(value_vectors.shape, F32),
            pltpu.SemaphoreType.DMA((2,)),
        ],
        [pl.BlockSpec(memory_space=pltpu.HBM)] * 2,
    )
    kv = []
    for g in range(groups):
        kv.append([own[g]])
        for k in range(1, n):
            kv[g].append(shifted(own[g], "ctx", k))

    prep_shapes = (
        pltpu.VMEM((rows, 3 * width), BF16),
        pltpu.VMEM((per_group * width, 3 * width), BF16),
        pltpu.VMEM((per_group, 2 * width, 2 * tokens), BF16),
        pltpu.VMEM((width, 2 * per_group * width), BF16),
        pltpu.VMEM((width, 2 * per_group * width), BF16),
        pltpu.VMEM((tokens, rows), F32),
        pltpu.VMEM((width, rows), F32),
        pltpu.VMEM((1, rows), F32),
        pltpu.VMEM((1, rows), F32),
    )
    prep = call(
        functools.partial(prep_kernel, cfg),
        tuple(shape for shape in prep_shapes for _ in range(groups)),
        (queries, query_feature, key_feature, *near(*own)),
    )
    attend_shapes = (
        pltpu.VMEM((2 * tokens, rows), F32),
        pltpu.VMEM((2, width, rows), BF16),
        pltpu.VMEM((1, rows), F32),
        pltpu.VMEM((per_group, 2 * width, tokens), F32),
    )
    scratch = [
        pltpu.VMEM((pairs, 2, 2 * tokens, width), F32),
        pltpu.VMEM((pairs, 2, 2 * tokens, width), F32),
        pltpu.VMEM((1, rows), F32),
        pltpu.VMEM((1, rows), F32),
        pltpu.VMEM((width, rows), F32),
        pltpu.VMEM((width, rows), F32),
        pltpu.VMEM((1, rows), F32),
        pltpu.VMEM((pairs, 2 * tokens, rows), F32),
        pltpu.VMEM((pairs, per_group, 2 * width, 2 * tokens), F32),
    ]
    for_query, mine = [], []
    for g in range(groups):
        q_3, wk_t, fq, wk_2, wq_2, *window = prep[g::groups]
        win, grad, gden, dfq, *grads = call(
            functools.partial(attend_kernel, cfg),
            attend_shapes + (kv_shape,) * (n - 2),
            near(q_3, wk_t, fq, wk_2, *window, *kv[g][1:]),
            scratch,
            megabytes=20,
        )
        soft, *near_grads = call(
            functools.partial(window_kernel, cfg),
            (pltpu.VMEM((2, 2 * tokens, rows), BF16), kv_shape, kv_shape),
            near(q_3, win, grad, gden, kv[g][0], kv[g][1]),
        )
        grads = near_grads + grads
        for_query.append((soft, dfq, fq, wq_2, kv[g][0], kv[g][1]))
        back = []
        for k in range(1, n):
            back.append(shifted(grads[k], "ctx", -k))
        mine.append(call(add_kernel, kv_shape, near(grads[0], *back)))
    query_grad = call(
        functools.partial(query_kernel, cfg),
        jax.ShapeDtypeStruct(queries.shape, F32),
        near(*[x for parts in zip(*for_query) for x in parts]),
    )
    other = [lax.ppermute(part, "sub", [(0, 1), (1, 0)]) for part in mine]
    key_grad, value_grad = call(
        functools.partial(place_kernel, cfg),
        (
            jax.ShapeDtypeStruct(key_vectors.shape, F32),
            jax.ShapeDtypeStruct(value_vectors.shape, F32),
        ),
        near(*mine, *other),
    )
    return query_grad, key_grad, value_grad


def solution(mesh):
    placed = (
        P(("groups", "ctx"), ("head", "sub"), None),
        P(("groups", "ctx"), "head", None),
        P(("groups", "ctx"), "head", None),
        P(("head", "sub"), None, None),
        P(("head", "sub"), None, None),
    )

    def step(queries, key_vectors, value_vectors, query_feature, key_feature):
        return jax.shard_map(
            layer,
            mesh=mesh,
            in_specs=placed,
            out_specs=placed[:3],
            check_vma=False,
        )(queries, key_vectors, value_vectors, query_feature, key_feature)

    return step
```

profile of v0, /device:TPU:0, one launch (start us, length us, event | category | flops | bytes accessed | tf_op | source)
XLA Modules:
  0.0 53.5 jit_solution(17711724040455083614)
XLA Ops:
  0.7 1.0 %copy-done.3 = f32[128,4,128]{2,1,0:T(4,128)S(1)} copy-done((f32[128,4,128]{2,1,0:T(4,128)S(1)}, f32[128,4,128]{2,1,0:T(4,128)}, u32[]{:S(2)}) %copy-start.3) | copy-done | bytes 262168
  1.7 0.9 %copy-done.4 = f32[128,4,128]{2,1,0:T(4,128)S(1)} copy-done((f32[128,4,128]{2,1,0:T(4,128)S(1)}, f32[128,4,128]{2,1,0:T(4,128)}, u32[]{:S(2)}) %copy-start.4) | copy-done | bytes 262168
  2.9 5.0 %collective-permute-start.3 = (f32[2,128,128]{2,1,0:T(8,128)S(1)}, f32[2,128,128]{2,1,0:T(8,128)S(1)}, u32[]{:S(2)}, u32[]{:S(2)}) collective-permute-start(f32[2,128,128]{2,1,0:T(8,128)S(1)} %get-tuple-element.44.refs_1_.refs_4_.refs_9_), channel_id=1, source_target_pairs={{0,4},{4,8},{8,12},{1,5},{5,9},{9,13},{2,6},{6,10},{10,14},{3,7},{... | collective-permute-start | bytes 393224 | tf_op jit(solution)/shard_map/ppermute | solution.py:23
  7.9 4.5 %collective-permute-start.4 = (f32[2,128,128]{2,1,0:T(8,128)S(1)}, f32[2,128,128]{2,1,0:T(8,128)S(1)}, u32[]{:S(2)}, u32[]{:S(2)}) collective-permute-start(f32[2,128,128]{2,1,0:T(8,128)S(1)} %get-tuple-element.44.refs_1_.refs_4_.refs_9_), channel_id=1, source_target_pairs={{0,8},{4,12},{1,9},{5,13},{2,10},{6,14},{3,11},{7,15},{16,24},{20,... | collective-permute-start | bytes 393224 | tf_op jit(solution)/shard_map/ppermute | solution.py:23
  12.4 1.3 %collective-permute-start.5 = (f32[2,128,128]{2,1,0:T(8,128)S(1)}, f32[2,128,128]{2,1,0:T(8,128)S(1)}, u32[]{:S(2)}, u32[]{:S(2)}) collective-permute-start(f32[2,128,128]{2,1,0:T(8,128)S(1)} %get-tuple-element.44.refs_1_.refs_4_.refs_9_), channel_id=1, source_target_pairs={{0,12},{1,13},{2,14},{3,15},{16,28},{17,29},{18,30},{19,31}} | collective-permute-start | bytes 393224 | tf_op jit(solution)/shard_map/ppermute | solution.py:23
  13.7 1.3 %collective-permute-start = (f32[2,128,128]{2,1,0:T(8,128)S(1)}, f32[2,128,128]{2,1,0:T(8,128)S(1)}, u32[]{:S(2)}, u32[]{:S(2)}) collective-permute-start(f32[2,128,128]{2,1,0:T(8,128)S(1)} %get-tuple-element.43.refs_0_.refs_4_.refs_8_), channel_id=1, source_target_pairs={{0,4},{4,8},{8,12},{1,5},{5,9},{9,13},{2,6},{6,10},{10,14},{3,7},{... | collective-permute-start | bytes 393224 | tf_op jit(solution)/shard_map/ppermute | solution.py:23
  15.0 1.3 %collective-permute-start.1 = (f32[2,128,128]{2,1,0:T(8,128)S(1)}, f32[2,128,128]{2,1,0:T(8,128)S(1)}, u32[]{:S(2)}, u32[]{:S(2)}) collective-permute-start(f32[2,128,128]{2,1,0:T(8,128)S(1)} %get-tuple-element.43.refs_0_.refs_4_.refs_8_), channel_id=1, source_target_pairs={{0,8},{4,12},{1,9},{5,13},{2,10},{6,14},{3,11},{7,15},{16,24},{20,... | collective-permute-start | bytes 393224 | tf_op jit(solution)/shard_map/ppermute | solution.py:23
  16.3 2.1 %collective-permute-start.2 = (f32[2,128,128]{2,1,0:T(8,128)S(1)}, f32[2,128,128]{2,1,0:T(8,128)S(1)}, u32[]{:S(2)}, u32[]{:S(2)}) collective-permute-start(f32[2,128,128]{2,1,0:T(8,128)S(1)} %get-tuple-element.43.refs_0_.refs_4_.refs_8_), channel_id=1, source_target_pairs={{0,12},{1,13},{2,14},{3,15},{16,28},{17,29},{18,30},{19,31}} | collective-permute-start | bytes 393224 | tf_op jit(solution)/shard_map/ppermute | solution.py:23
  18.5 1.0 %copy-done.1 = f32[8,128,128]{2,1,0:T(8,128)S(1)} copy-done((f32[8,128,128]{2,1,0:T(8,128)S(1)}, f32[8,128,128]{2,1,0:T(8,128)}, u32[]{:S(2)}) %copy-start.1) | copy-done | bytes 524312
  19.5 1.0 %copy-done.2 = f32[8,128,128]{2,1,0:T(8,128)S(1)} copy-done((f32[8,128,128]{2,1,0:T(8,128)S(1)}, f32[8,128,128]{2,1,0:T(8,128)}, u32[]{:S(2)}) %copy-start.2) | copy-done | bytes 524312
  20.5 2.3 %shard_map.77 = (bf16[512,384]{1,0:T(8,128)(2,1)S(1)}, bf16[512,384]{1,0:T(8,128)(2,1)S(1)}, bf16[512,384]{1,0:T(8,128)(2,1)S(1)}, bf16[512,384]{1,0:T(8,128)(2,...) custom-call(f32[128,8,128]{2,1,0:T(8,128)S(1)} %copy-done, ...), custom_call_target="tpu_custom_call" | custom-call | tf_op jit(solution)/shard_map/pallas_call | solution.py:357
  22.9 0.9 %shard_map.80 = (f32[256,512]{1,0:T(8,128)S(1)}, bf16[2,128,512]{2,1,0:T(8,128)(2,1)S(1)}, f32[1,512]{1,0:T(1,128)S(1)}, f32[4,256,128]{2,1,0:T(8,128)S(1)}, f32...) custom-call(bf16[512,384]{1,0:T(8,128)(2,1)S(1)} %get-tuple-element.57.refs_0_, ...), custom_call_target="tpu_custom_call" | custom-call | tf_op jit(solution)/shard_map/pallas_call | solution.py:357
  24.5 1.3 %collective-permute-start.9 = (f32[2,128,128]{2,1,0:T(8,128)S(1)}, f32[2,128,128]{2,1,0:T(8,128)S(1)}, u32[]{:S(2)}, u32[]{:S(2)}) collective-permute-start(f32[2,128,128]{2,1,0:T(8,128)S(1)} %get-tuple-element.78), channel_id=1, source_target_pairs={{4,0},{8,4},{12,8},{5,1},{9,5},{13,9},{6,2},{10,6},{14,10},{7,3},{... | collective-permute-start | bytes 393224 | tf_op jit(solution)/shard_map/ppermute | solution.py:23
  25.8 1.3 %collective-permute-start.10 = (f32[2,128,128]{2,1,0:T(8,128)S(1)}, f32[2,128,128]{2,1,0:T(8,128)S(1)}, u32[]{:S(2)}, u32[]{:S(2)}) collective-permute-start(f32[2,128,128]{2,1,0:T(8,128)S(1)} %get-tuple-element.79), channel_id=1, source_target_pairs={{8,0},{12,4},{9,1},{13,5},{10,2},{14,6},{11,3},{15,7},{24,16},{28,... | collective-permute-start | bytes 393224 | tf_op jit(solution)/shard_map/ppermute | solution.py:23
  27.1 1.3 %collective-permute-start.11 = (f32[2,128,128]{2,1,0:T(8,128)S(1)}, f32[2,128,128]{2,1,0:T(8,128)S(1)}, u32[]{:S(2)}, u32[]{:S(2)}) collective-permute-start(f32[2,128,128]{2,1,0:T(8,128)S(1)} %get-tuple-element.80), channel_id=1, source_target_pairs={{12,0},{13,1},{14,2},{15,3},{28,16},{29,17},{30,18},{31,19}} | collective-permute-start | bytes 393224 | tf_op jit(solution)/shard_map/ppermute | solution.py:23
  28.4 0.9 %shard_map.78 = (f32[256,512]{1,0:T(8,128)S(1)}, bf16[2,128,512]{2,1,0:T(8,128)(2,1)S(1)}, f32[1,512]{1,0:T(1,128)S(1)}, f32[4,256,128]{2,1,0:T(8,128)S(1)}, f32...) custom-call(bf16[512,384]{1,0:T(8,128)(2,1)S(1)} %get-tuple-element.45.refs_0_, ...), custom_call_target="tpu_custom_call" | custom-call | tf_op jit(solution)/shard_map/pallas_call | solution.py:357
  30.0 1.3 %collective-permute-start.6 = (f32[2,128,128]{2,1,0:T(8,128)S(1)}, f32[2,128,128]{2,1,0:T(8,128)S(1)}, u32[]{:S(2)}, u32[]{:S(2)}) collective-permute-start(f32[2,128,128]{2,1,0:T(8,128)S(1)} %get-tuple-element.74), channel_id=1, source_target_pairs={{4,0},{8,4},{12,8},{5,1},{9,5},{13,9},{6,2},{10,6},{14,10},{7,3},{... | collective-permute-start | bytes 393224 | tf_op jit(solution)/shard_map/ppermute | solution.py:23
  31.3 1.3 %collective-permute-start.7 = (f32[2,128,128]{2,1,0:T(8,128)S(1)}, f32[2,128,128]{2,1,0:T(8,128)S(1)}, u32[]{:S(2)}, u32[]{:S(2)}) collective-permute-start(f32[2,128,128]{2,1,0:T(8,128)S(1)} %get-tuple-element.75), channel_id=1, source_target_pairs={{8,0},{12,4},{9,1},{13,5},{10,2},{14,6},{11,3},{15,7},{24,16},{28,... | collective-permute-start | bytes 393224 | tf_op jit(solution)/shard_map/ppermute | solution.py:23
  32.6 1.3 %collective-permute-start.8 = (f32[2,128,128]{2,1,0:T(8,128)S(1)}, f32[2,128,128]{2,1,0:T(8,128)S(1)}, u32[]{:S(2)}, u32[]{:S(2)}) collective-permute-start(f32[2,128,128]{2,1,0:T(8,128)S(1)} %get-tuple-element.76), channel_id=1, source_target_pairs={{12,0},{13,1},{14,2},{15,3},{28,16},{29,17},{30,18},{31,19}} | collective-permute-start | bytes 393224 | tf_op jit(solution)/shard_map/ppermute | solution.py:23
  33.9 5.9 %collective-permute-done.10.refs_2_ = f32[2,128,128]{2,1,0:T(8,128)S(1)} collective-permute-done((f32[2,128,128]{2,1,0:T(8,128)S(1)}, f32[2,128,128]{2,1,0:T(8,128)S(1)}, u32[]{:S(2)}, u32[]{:S(2)}) %collective-permute-start.10) | collective-permute-done | bytes 131104 | tf_op jit(solution)/shard_map/ppermute | solution.py:23
  40.0 1.0 %collective-permute-done.6.refs_1_ = f32[2,128,128]{2,1,0:T(8,128)S(1)} collective-permute-done((f32[2,128,128]{2,1,0:T(8,128)S(1)}, f32[2,128,128]{2,1,0:T(8,128)S(1)}, u32[]{:S(2)}, u32[]{:S(2)}) %collective-permute-start.6) | collective-permute-done | bytes 131104 | tf_op jit(solution)/shard_map/ppermute | solution.py:23
  40.9 9.6 %collective-permute-done.7.refs_2_ = f32[2,128,128]{2,1,0:T(8,128)S(1)} collective-permute-done((f32[2,128,128]{2,1,0:T(8,128)S(1)}, f32[2,128,128]{2,1,0:T(8,128)S(1)}, u32[]{:S(2)}, u32[]{:S(2)}) %collective-permute-start.7) | collective-permute-done | bytes 131104 | tf_op jit(solution)/shard_map/ppermute | solution.py:23
  50.7 1.8 %shard_map.82 = f32[128,8,128]{2,1,0:T(8,128)} custom-call(bf16[2,256,512]{2,1,0:T(8,128)(2,1)S(1)} %get-tuple-element.56.refs_0_, bf16[2,256,512]{2,1,0:T(8,128)(2,1)S(1)} %get-tuple-element.68.refs_1_, f32[4,256,128]{2,1,0:T(8,128)S(1)} %get-tuple-element.69.refs_2_, f32[4,256,128]{2,1,0:T(8,128)S(1)} %get-tuple-element.70.refs_3_, ...), custom_call_target="tpu_custom_call" | custom-call | tf_op jit(solution)/shard_map/pallas_call | solution.py:357
  52.5 1.0 %shard_map.85 = (f32[128,4,128]{2,1,0:T(4,128)}, f32[128,4,128]{2,1,0:T(4,128)}) custom-call(f32[2,128,128]{2,1,0:T(8,128)S(1)} %shard_map.83.refs_0_, f32[2,128,128]{2,1,0:T(8,128)S(1)} %shard_map.84.refs_1_, f32[2,128,128]{2,1,0:T(8,128)S(1)} %collective-permute-done.12.refs_2_, f32[2,128,128]{2,1,0:T(8,128)S(1)} %collective-permute-done.13.refs_3_), custom_call_target="tpu_custom_call" | custom-call | tf_op jit(solution)/shard_map/pallas_call | solution.py:357
  (24 shorter events, 2.0 us)
Async XLA Ops:
  0.6 17.8 %copy-start = (f32[128,8,128]{2,1,0:T(8,128)S(1)}, f32[128,8,128]{2,1,0:T(8,128)}, u32[]{:S(2)}) copy-start(f32[128,8,128]{2,1,0:T(8,128)} %q_ref.1) | copy-start | bytes 1572868
  0.6 1.0 %copy-start.3 = (f32[128,4,128]{2,1,0:T(4,128)S(1)}, f32[128,4,128]{2,1,0:T(4,128)}, u32[]{:S(2)}) copy-start(f32[128,4,128]{2,1,0:T(4,128)} %k_hbm.1) | copy-start | bytes 786436
  1.6 0.9 %copy-start.4 = (f32[128,4,128]{2,1,0:T(4,128)S(1)}, f32[128,4,128]{2,1,0:T(4,128)}, u32[]{:S(2)}) copy-start(f32[128,4,128]{2,1,0:T(4,128)} %v_hbm.1) | copy-start | bytes 786436
  2.9 13.4 %collective-permute-start.3 = (f32[2,128,128]{2,1,0:T(8,128)S(1)}, f32[2,128,128]{2,1,0:T(8,128)S(1)}, u32[]{:S(2)}, u32[]{:S(2)}) collective-permute-start(f32[2,128,128]{2,1,0:T(8,128)S(1)} %get-tuple-element.44.refs_1_.refs_4_.refs_9_), channel_id=1, source_target_pairs={{0,4},{4,8},{8,12},{1,5},{5,9},{9,13},{2,6},{6,10},{10,14},{3,7},{... | collective-permute-start | bytes 393224 | tf_op jit(solution)/shard_map/ppermute | solution.py:23
  7.9 15.0 %collective-permute-start.4 = (f32[2,128,128]{2,1,0:T(8,128)S(1)}, f32[2,128,128]{2,1,0:T(8,128)S(1)}, u32[]{:S(2)}, u32[]{:S(2)}) collective-permute-start(f32[2,128,128]{2,1,0:T(8,128)S(1)} %get-tuple-element.44.refs_1_.refs_4_.refs_9_), channel_id=1, source_target_pairs={{0,8},{4,12},{1,9},{5,13},{2,10},{6,14},{3,11},{7,15},{16,24},{20,... | collective-permute-start | bytes 393224 | tf_op jit(solution)/shard_map/ppermute | solution.py:23
  12.4 10.5 %collective-permute-start.5 = (f32[2,128,128]{2,1,0:T(8,128)S(1)}, f32[2,128,128]{2,1,0:T(8,128)S(1)}, u32[]{:S(2)}, u32[]{:S(2)}) collective-permute-start(f32[2,128,128]{2,1,0:T(8,128)S(1)} %get-tuple-element.44.refs_1_.refs_4_.refs_9_), channel_id=1, source_target_pairs={{0,12},{1,13},{2,14},{3,15},{16,28},{17,29},{18,30},{19,31}} | collective-permute-start | bytes 393224 | tf_op jit(solution)/shard_map/ppermute | solution.py:23
  13.7 13.4 %collective-permute-start = (f32[2,128,128]{2,1,0:T(8,128)S(1)}, f32[2,128,128]{2,1,0:T(8,128)S(1)}, u32[]{:S(2)}, u32[]{:S(2)}) collective-permute-start(f32[2,128,128]{2,1,0:T(8,128)S(1)} %get-tuple-element.43.refs_0_.refs_4_.refs_8_), channel_id=1, source_target_pairs={{0,4},{4,8},{8,12},{1,5},{5,9},{9,13},{2,6},{6,10},{10,14},{3,7},{... | collective-permute-start | bytes 393224 | tf_op jit(solution)/shard_map/ppermute | solution.py:23
  15.0 13.4 %collective-permute-start.1 = (f32[2,128,128]{2,1,0:T(8,128)S(1)}, f32[2,128,128]{2,1,0:T(8,128)S(1)}, u32[]{:S(2)}, u32[]{:S(2)}) collective-permute-start(f32[2,128,128]{2,1,0:T(8,128)S(1)} %get-tuple-element.43.refs_0_.refs_4_.refs_8_), channel_id=1, source_target_pairs={{0,8},{4,12},{1,9},{5,13},{2,10},{6,14},{3,11},{7,15},{16,24},{20,... | collective-permute-start | bytes 393224 | tf_op jit(solution)/shard_map/ppermute | solution.py:23
  16.3 12.1 %collective-permute-start.2 = (f32[2,128,128]{2,1,0:T(8,128)S(1)}, f32[2,128,128]{2,1,0:T(8,128)S(1)}, u32[]{:S(2)}, u32[]{:S(2)}) collective-permute-start(f32[2,128,128]{2,1,0:T(8,128)S(1)} %get-tuple-element.43.refs_0_.refs_4_.refs_8_), channel_id=1, source_target_pairs={{0,12},{1,13},{2,14},{3,15},{16,28},{17,29},{18,30},{19,31}} | collective-permute-start | bytes 393224 | tf_op jit(solution)/shard_map/ppermute | solution.py:23
  18.5 1.0 %copy-start.1 = (f32[8,128,128]{2,1,0:T(8,128)S(1)}, f32[8,128,128]{2,1,0:T(8,128)}, u32[]{:S(2)}) copy-start(f32[8,128,128]{2,1,0:T(8,128)} %wq_ref.1) | copy-start | bytes 1572868
  19.5 1.0 %copy-start.2 = (f32[8,128,128]{2,1,0:T(8,128)S(1)}, f32[8,128,128]{2,1,0:T(8,128)}, u32[]{:S(2)}) copy-start(f32[8,128,128]{2,1,0:T(8,128)} %wk_ref.1) | copy-start | bytes 1572868
  24.5 8.1 %collective-permute-start.9 = (f32[2,128,128]{2,1,0:T(8,128)S(1)}, f32[2,128,128]{2,1,0:T(8,128)S(1)}, u32[]{:S(2)}, u32[]{:S(2)}) collective-permute-start(f32[2,128,128]{2,1,0:T(8,128)S(1)} %get-tuple-element.78), channel_id=1, source_target_pairs={{4,0},{8,4},{12,8},{5,1},{9,5},{13,9},{6,2},{10,6},{14,10},{7,3},{... | collective-permute-start | bytes 393224 | tf_op jit(solution)/shard_map/ppermute | solution.py:23
  25.8 14.1 %collective-permute-start.10 = (f32[2,128,128]{2,1,0:T(8,128)S(1)}, f32[2,128,128]{2,1,0:T(8,128)S(1)}, u32[]{:S(2)}, u32[]{:S(2)}) collective-permute-start(f32[2,128,128]{2,1,0:T(8,128)S(1)} %get-tuple-element.79), channel_id=1, source_target_pairs={{8,0},{12,4},{9,1},{13,5},{10,2},{14,6},{11,3},{15,7},{24,16},{28,... | collective-permute-start | bytes 393224 | tf_op jit(solution)/shard_map/ppermute | solution.py:23
  27.1 12.7 %collective-permute-start.11 = (f32[2,128,128]{2,1,0:T(8,128)S(1)}, f32[2,128,128]{2,1,0:T(8,128)S(1)}, u32[]{:S(2)}, u32[]{:S(2)}) collective-permute-start(f32[2,128,128]{2,1,0:T(8,128)S(1)} %get-tuple-element.80), channel_id=1, source_target_pairs={{12,0},{13,1},{14,2},{15,3},{28,16},{29,17},{30,18},{31,19}} | collective-permute-start | bytes 393224 | tf_op jit(solution)/shard_map/ppermute | solution.py:23
  30.0 10.9 %collective-permute-start.6 = (f32[2,128,128]{2,1,0:T(8,128)S(1)}, f32[2,128,128]{2,1,0:T(8,128)S(1)}, u32[]{:S(2)}, u32[]{:S(2)}) collective-permute-start(f32[2,128,128]{2,1,0:T(8,128)S(1)} %get-tuple-element.74), channel_id=1, source_target_pairs={{4,0},{8,4},{12,8},{5,1},{9,5},{13,9},{6,2},{10,6},{14,10},{7,3},{... | collective-permute-start | bytes 393224 | tf_op jit(solution)/shard_map/ppermute | solution.py:23
  31.3 19.3 %collective-permute-start.7 = (f32[2,128,128]{2,1,0:T(8,128)S(1)}, f32[2,128,128]{2,1,0:T(8,128)S(1)}, u32[]{:S(2)}, u32[]{:S(2)}) collective-permute-start(f32[2,128,128]{2,1,0:T(8,128)S(1)} %get-tuple-element.75), channel_id=1, source_target_pairs={{8,0},{12,4},{9,1},{13,5},{10,2},{14,6},{11,3},{15,7},{24,16},{28,... | collective-permute-start | bytes 393224 | tf_op jit(solution)/shard_map/ppermute | solution.py:23
  32.6 18.0 %collective-permute-start.8 = (f32[2,128,128]{2,1,0:T(8,128)S(1)}, f32[2,128,128]{2,1,0:T(8,128)S(1)}, u32[]{:S(2)}, u32[]{:S(2)}) collective-permute-start(f32[2,128,128]{2,1,0:T(8,128)S(1)} %get-tuple-element.76), channel_id=1, source_target_pairs={{12,0},{13,1},{14,2},{15,3},{28,16},{29,17},{30,18},{31,19}} | collective-permute-start | bytes 393224 | tf_op jit(solution)/shard_map/ppermute | solution.py:23
  39.9 12.6 %collective-permute-start.13 = (f32[2,128,128]{2,1,0:T(8,128)S(1)}, f32[2,128,128]{2,1,0:T(8,128)S(1)}, u32[]{:S(2)}, u32[]{:S(2)}) collective-permute-start(f32[2,128,128]{2,1,0:T(8,128)S(1)} %shard_map.84.refs_1_), channel_id=1, source_target_pairs={{0,1},{1,0},{2,3},{3,2},{4,5},{5,4},{6,7},{7,6},{8,9},{9,8},{10,11... | collective-permute-start | bytes 393224 | tf_op jit(solution)/shard_map/ppermute | solution.py:449
  50.6 1.9 %collective-permute-start.12 = (f32[2,128,128]{2,1,0:T(8,128)S(1)}, f32[2,128,128]{2,1,0:T(8,128)S(1)}, u32[]{:S(2)}, u32[]{:S(2)}) collective-permute-start(f32[2,128,128]{2,1,0:T(8,128)S(1)} %shard_map.83.refs_0_), channel_id=1, source_target_pairs={{0,1},{1,0},{2,3},{3,2},{4,5},{5,4},{6,7},{7,6},{8,9},{9,8},{10,11... | collective-permute-start | bytes 393224 | tf_op jit(solution)/shard_map/ppermute | solution.py:449
where the time goes:
time: 54 us; the launch traced here: 53.5 us
  starting transfers between devices  23.4 us (43%)
  waiting for transfers between devices  16.6 us (31%)
  Pallas kernels  8.67 us (16%)
  local copies, waits for them, and re-layouts  4.03 us (7%)
  between operations  0.88 us (2%)
    ppermute x12, starting transfers between devices, shifted(): lax.ppermute(value, axis, [(i, i + steps) for i in range(first, last)])  23.2 us
    ppermute x12, waiting for transfers between devices, shifted(): lax.ppermute(value, axis, [(i, i + steps) for i in range(first, last)])  16.6 us
    pallas_call x10, Pallas kernels, call(): pl.pallas_call(kernel, out_shape=outs, in_specs=ins or [VMEM] * len(args)...  8.67 us
    unnamed x10, local copies, waits for them, and re-layouts  4.03 us
  transfers between devices with their start and end apart: 14, of which 3 were waited for; matrix products, arithmetic and copies ran while one was open for 0% of the time, Pallas kernels for 14%

commit v1 on v0

--- a/solution.py
+++ b/solution.py
@@ -115,8 +115,17 @@
             kv_ref[slot] = value
 
 
-def prep_kernel(cfg, q_ref, wq_ref, wk_ref, *refs):
-    own_refs, outs = refs[: cfg.groups], refs[cfg.groups :]
+def prep_kernel(cfg, *refs):
+    sources, own_refs, outs = refs[:3], refs[3 : 3 + cfg.groups], refs[3 + cfg.groups : -4]
+    q_ref, wq_ref, wk_ref, sems = refs[-4:]
+    copies = [
+        pltpu.make_async_copy(src, dst, sems.at[i])
+        for i, (src, dst) in enumerate(zip(sources, (q_ref, wq_ref, wk_ref)))
+    ]
+    for copy in copies:
+        copy.start()
+    for copy in copies:
+        copy.wait()
     tokens, width, per_group = cfg.tokens, cfg.width, cfg.per_group
     rows = per_group * tokens
     scale = 1.0 / math.sqrt(width)
@@ -353,6 +362,10 @@
     return [pltpu.with_memory_space_constraint(x, pltpu.VMEM) for x in arrays]
 
 
+def far_off(*arrays):
+    return [pltpu.with_memory_space_constraint(x, pltpu.HBM) for x in arrays]
+
+
 def call(kernel, outs, args, scratch=(), ins=None, megabytes=16):
     return pl.pallas_call(
         kernel,
@@ -373,13 +386,13 @@
     own = call(
         functools.partial(pack_kernel, cfg),
         (kv_shape,) * groups,
-        (key_vectors, value_vectors),
+        far_off(key_vectors, value_vectors),
         [
             pltpu.VMEM(key_vectors.shape, F32),
             pltpu.VMEM(value_vectors.shape, F32),
             pltpu.SemaphoreType.DMA((2,)),
         ],
-        [pl.BlockSpec(memory_space=pltpu.HBM)] * 2,
+        [pl.BlockSpec(memory_space=pl.ANY)] * 2,
     )
     kv = []
     for g in range(groups):
@@ -401,7 +414,14 @@
     prep = call(
         functools.partial(prep_kernel, cfg),
         tuple(shape for shape in prep_shapes for _ in range(groups)),
-        (queries, query_feature, key_feature, *near(*own)),
+        far_off(queries, query_feature, key_feature) + near(*own),
+        [
+            pltpu.VMEM(queries.shape, F32),
+            pltpu.VMEM(query_feature.shape, F32),
+            pltpu.VMEM(key_feature.shape, F32),
+            pltpu.SemaphoreType.DMA((3,)),
+        ],
+        [pl.BlockSpec(memory_space=pl.ANY)] * 3 + [VMEM] * groups,
     )
     attend_shapes = (
         pltpu.VMEM((2 * tokens, rows), F32),

time: 54 us -> 52.4 us (0.970)
  local copies, waits for them, and re-layouts: 4.03 us -> 0 us
  Pallas kernels: 8.67 us -> 11.1 us
    unnamed x10 -> x0, local copies, waits for them, and re-layouts: 4.03 us -> none
    pallas_call x10, Pallas kernels: 8.67 us -> 11.1 us  [call(): pl.pallas_call(kernel, out_shape=outs, in_specs=ins or [VMEM] * len(args)...]
  transfers between devices with their start and end apart: 14 -> 14, of which waited for: 3 -> 3; matrix products, arithmetic and copies ran while one was open for 0% -> 0% of each run, Pallas kernels for 14% -> 17%
where the time goes in v1:
time: 52.4 us; the launch traced here: 52 us
  starting transfers between devices  23.4 us (45%)
  waiting for transfers between devices  16.7 us (32%)
  Pallas kernels  11.1 us (21%)
  between operations  0.85 us (2%)
    ppermute x12, starting transfers between devices, shifted(): lax.ppermute(value, axis, [(i, i + steps) for i in range(first, last)])  23.2 us
    ppermute x12, waiting for transfers between devices, shifted(): lax.ppermute(value, axis, [(i, i + steps) for i in range(first, last)])  16.7 us
    pallas_call x10, Pallas kernels, call(): pl.pallas_call(kernel, out_shape=outs, in_specs=ins or [VMEM] * len(args)...  11.1 us
  transfers between devices with their start and end apart: 14, of which 3 were waited for; matrix products, arithmetic and copies ran while one was open for 0% of the time, Pallas kernels for 17%

profile of v1, /device:TPU:0, one launch (start us, length us, event | category | flops | bytes accessed | tf_op | source)
XLA Modules:
  0.0 52.0 jit_solution(1075995304710558773)
XLA Ops:
  0.6 1.2 %shard_map.76 = (f32[2,128,128]{2,1,0:T(8,128)S(1)}, f32[2,128,128]{2,1,0:T(8,128)S(1)}) custom-call(f32[128,4,128]{2,1,0:T(4,128)} %k_hbm.1, f32[128,4,128]{2,1,0:T(4,128)} %v_hbm.1), custom_call_target="tpu_custom_call" | custom-call | tf_op jit(solution)/shard_map/pallas_call | solution.py:370
  1.9 5.0 %collective-permute-start.3 = (f32[2,128,128]{2,1,0:T(8,128)S(1)}, f32[2,128,128]{2,1,0:T(8,128)S(1)}, u32[]{:S(2)}, u32[]{:S(2)}) collective-permute-start(f32[2,128,128]{2,1,0:T(8,128)S(1)} %get-tuple-element.44.refs_4_.refs_9_), channel_id=1, source_target_pairs={{0,4},{4,8},{8,12},{1,5},{5,9},{9,13},{2,6},{6,10},{10,14},{3,7},{... | collective-permute-start | bytes 393224 | tf_op jit(solution)/shard_map/ppermute | solution.py:23
  6.8 4.5 %collective-permute-start.4 = (f32[2,128,128]{2,1,0:T(8,128)S(1)}, f32[2,128,128]{2,1,0:T(8,128)S(1)}, u32[]{:S(2)}, u32[]{:S(2)}) collective-permute-start(f32[2,128,128]{2,1,0:T(8,128)S(1)} %get-tuple-element.44.refs_4_.refs_9_), channel_id=1, source_target_pairs={{0,8},{4,12},{1,9},{5,13},{2,10},{6,14},{3,11},{7,15},{16,24},{20,... | collective-permute-start | bytes 393224 | tf_op jit(solution)/shard_map/ppermute | solution.py:23
  11.3 1.3 %collective-permute-start.5 = (f32[2,128,128]{2,1,0:T(8,128)S(1)}, f32[2,128,128]{2,1,0:T(8,128)S(1)}, u32[]{:S(2)}, u32[]{:S(2)}) collective-permute-start(f32[2,128,128]{2,1,0:T(8,128)S(1)} %get-tuple-element.44.refs_4_.refs_9_), channel_id=1, source_target_pairs={{0,12},{1,13},{2,14},{3,15},{16,28},{17,29},{18,30},{19,31}} | collective-permute-start | bytes 393224 | tf_op jit(solution)/shard_map/ppermute | solution.py:23
  12.6 1.3 %collective-permute-start = (f32[2,128,128]{2,1,0:T(8,128)S(1)}, f32[2,128,128]{2,1,0:T(8,128)S(1)}, u32[]{:S(2)}, u32[]{:S(2)}) collective-permute-start(f32[2,128,128]{2,1,0:T(8,128)S(1)} %get-tuple-element.43.refs_3_.refs_4_.refs_8_), channel_id=1, source_target_pairs={{0,4},{4,8},{8,12},{1,5},{5,9},{9,13},{2,6},{6,10},{10,14},{3,7},{... | collective-permute-start | bytes 393224 | tf_op jit(solution)/shard_map/ppermute | solution.py:23
  13.9 1.3 %collective-permute-start.1 = (f32[2,128,128]{2,1,0:T(8,128)S(1)}, f32[2,128,128]{2,1,0:T(8,128)S(1)}, u32[]{:S(2)}, u32[]{:S(2)}) collective-permute-start(f32[2,128,128]{2,1,0:T(8,128)S(1)} %get-tuple-element.43.refs_3_.refs_4_.refs_8_), channel_id=1, source_target_pairs={{0,8},{4,12},{1,9},{5,13},{2,10},{6,14},{3,11},{7,15},{16,24},{20,... | collective-permute-start | bytes 393224 | tf_op jit(solution)/shard_map/ppermute | solution.py:23
  15.3 2.1 %collective-permute-start.2 = (f32[2,128,128]{2,1,0:T(8,128)S(1)}, f32[2,128,128]{2,1,0:T(8,128)S(1)}, u32[]{:S(2)}, u32[]{:S(2)}) collective-permute-start(f32[2,128,128]{2,1,0:T(8,128)S(1)} %get-tuple-element.43.refs_3_.refs_4_.refs_8_), channel_id=1, source_target_pairs={{0,12},{1,13},{2,14},{3,15},{16,28},{17,29},{18,30},{19,31}} | collective-permute-start | bytes 393224 | tf_op jit(solution)/shard_map/ppermute | solution.py:23
  17.4 3.9 %shard_map.77 = (bf16[512,384]{1,0:T(8,128)(2,1)S(1)}, bf16[512,384]{1,0:T(8,128)(2,1)S(1)}, bf16[512,384]{1,0:T(8,128)(2,1)S(1)}, bf16[512,384]{1,0:T(8,128)(2,...) custom-call(f32[128,8,128]{2,1,0:T(8,128)} %refs_0_.1, ...), custom_call_target="tpu_custom_call" | custom-call | tf_op jit(solution)/shard_map/pallas_call | solution.py:370
  21.3 0.9 %shard_map.80 = (f32[256,512]{1,0:T(8,128)S(1)}, bf16[2,128,512]{2,1,0:T(8,128)(2,1)S(1)}, f32[1,512]{1,0:T(1,128)S(1)}, f32[4,256,128]{2,1,0:T(8,128)S(1)}, f32...) custom-call(bf16[512,384]{1,0:T(8,128)(2,1)S(1)} %get-tuple-element.57.refs_0_, ...), custom_call_target="tpu_custom_call" | custom-call | tf_op jit(solution)/shard_map/pallas_call | solution.py:370
  22.1 0.7 %shard_map.81 = (bf16[2,256,512]{2,1,0:T(8,128)(2,1)S(1)}, f32[2,128,128]{2,1,0:T(8,128)S(1)}, f32[2,128,128]{2,1,0:T(8,128)S(1)}) custom-call(bf16[512,384]{1,0:T(8,128)(2,1)S(1)} %get-tuple-element.57.refs_0_, f32[256,512]{1,0:T(8,128)S(1)} %get-tuple-element.65.refs_1_, bf16[2,128,512]{2,1,0:T(8,128)(2,1)S(1)} %get-tuple-element.66.refs_2_, ...), custom_call_target="tpu_custom_call" | custom-call | tf_op jit(solution)/shard_map/pallas_call | solution.py:370
  22.8 1.3 %collective-permute-start.9 = (f32[2,128,128]{2,1,0:T(8,128)S(1)}, f32[2,128,128]{2,1,0:T(8,128)S(1)}, u32[]{:S(2)}, u32[]{:S(2)}) collective-permute-start(f32[2,128,128]{2,1,0:T(8,128)S(1)} %get-tuple-element.78), channel_id=1, source_target_pairs={{4,0},{8,4},{12,8},{5,1},{9,5},{13,9},{6,2},{10,6},{14,10},{7,3},{... | collective-permute-start | bytes 393224 | tf_op jit(solution)/shard_map/ppermute | solution.py:23
  24.1 1.3 %collective-permute-start.10 = (f32[2,128,128]{2,1,0:T(8,128)S(1)}, f32[2,128,128]{2,1,0:T(8,128)S(1)}, u32[]{:S(2)}, u32[]{:S(2)}) collective-permute-start(f32[2,128,128]{2,1,0:T(8,128)S(1)} %get-tuple-element.79), channel_id=1, source_target_pairs={{8,0},{12,4},{9,1},{13,5},{10,2},{14,6},{11,3},{15,7},{24,16},{28,... | collective-permute-start | bytes 393224 | tf_op jit(solution)/shard_map/ppermute | solution.py:23
  25.5 1.3 %collective-permute-start.11 = (f32[2,128,128]{2,1,0:T(8,128)S(1)}, f32[2,128,128]{2,1,0:T(8,128)S(1)}, u32[]{:S(2)}, u32[]{:S(2)}) collective-permute-start(f32[2,128,128]{2,1,0:T(8,128)S(1)} %get-tuple-element.80), channel_id=1, source_target_pairs={{12,0},{13,1},{14,2},{15,3},{28,16},{29,17},{30,18},{31,19}} | collective-permute-start | bytes 393224 | tf_op jit(solution)/shard_map/ppermute | solution.py:23
  26.8 0.9 %shard_map.78 = (f32[256,512]{1,0:T(8,128)S(1)}, bf16[2,128,512]{2,1,0:T(8,128)(2,1)S(1)}, f32[1,512]{1,0:T(1,128)S(1)}, f32[4,256,128]{2,1,0:T(8,128)S(1)}, f32...) custom-call(bf16[512,384]{1,0:T(8,128)(2,1)S(1)} %get-tuple-element.45.refs_0_, ...), custom_call_target="tpu_custom_call" | custom-call | tf_op jit(solution)/shard_map/pallas_call | solution.py:370
  27.7 0.7 %shard_map.79 = (bf16[2,256,512]{2,1,0:T(8,128)(2,1)S(1)}, f32[2,128,128]{2,1,0:T(8,128)S(1)}, f32[2,128,128]{2,1,0:T(8,128)S(1)}) custom-call(bf16[512,384]{1,0:T(8,128)(2,1)S(1)} %get-tuple-element.45.refs_0_, f32[256,512]{1,0:T(8,128)S(1)} %get-tuple-element.53.refs_1_, bf16[2,128,512]{2,1,0:T(8,128)(2,1)S(1)} %get-tuple-element.54.refs_2_, ...), custom_call_target="tpu_custom_call" | custom-call | tf_op jit(solution)/shard_map/pallas_call | solution.py:370
  28.4 1.3 %collective-permute-start.6 = (f32[2,128,128]{2,1,0:T(8,128)S(1)}, f32[2,128,128]{2,1,0:T(8,128)S(1)}, u32[]{:S(2)}, u32[]{:S(2)}) collective-permute-start(f32[2,128,128]{2,1,0:T(8,128)S(1)} %get-tuple-element.74), channel_id=1, source_target_pairs={{4,0},{8,4},{12,8},{5,1},{9,5},{13,9},{6,2},{10,6},{14,10},{7,3},{... | collective-permute-start | bytes 393224 | tf_op jit(solution)/shard_map/ppermute | solution.py:23
  29.7 1.3 %collective-permute-start.7 = (f32[2,128,128]{2,1,0:T(8,128)S(1)}, f32[2,128,128]{2,1,0:T(8,128)S(1)}, u32[]{:S(2)}, u32[]{:S(2)}) collective-permute-start(f32[2,128,128]{2,1,0:T(8,128)S(1)} %get-tuple-element.75), channel_id=1, source_target_pairs={{8,0},{12,4},{9,1},{13,5},{10,2},{14,6},{11,3},{15,7},{24,16},{28,... | collective-permute-start | bytes 393224 | tf_op jit(solution)/shard_map/ppermute | solution.py:23
  31.0 1.3 %collective-permute-start.8 = (f32[2,128,128]{2,1,0:T(8,128)S(1)}, f32[2,128,128]{2,1,0:T(8,128)S(1)}, u32[]{:S(2)}, u32[]{:S(2)}) collective-permute-start(f32[2,128,128]{2,1,0:T(8,128)S(1)} %get-tuple-element.76), channel_id=1, source_target_pairs={{12,0},{13,1},{14,2},{15,3},{28,16},{29,17},{30,18},{31,19}} | collective-permute-start | bytes 393224 | tf_op jit(solution)/shard_map/ppermute | solution.py:23
  32.3 5.5 %collective-permute-done.10.refs_2_ = f32[2,128,128]{2,1,0:T(8,128)S(1)} collective-permute-done((f32[2,128,128]{2,1,0:T(8,128)S(1)}, f32[2,128,128]{2,1,0:T(8,128)S(1)}, u32[]{:S(2)}, u32[]{:S(2)}) %collective-permute-start.10) | collective-permute-done | bytes 131104 | tf_op jit(solution)/shard_map/ppermute | solution.py:23
  37.8 0.1 collective-permute-start.13
  37.9 2.6 %collective-permute-done.6.refs_1_ = f32[2,128,128]{2,1,0:T(8,128)S(1)} collective-permute-done((f32[2,128,128]{2,1,0:T(8,128)S(1)}, f32[2,128,128]{2,1,0:T(8,128)S(1)}, u32[]{:S(2)}, u32[]{:S(2)}) %collective-permute-start.6) | collective-permute-done | bytes 131104 | tf_op jit(solution)/shard_map/ppermute | solution.py:23
  40.4 8.6 %collective-permute-done.7.refs_2_ = f32[2,128,128]{2,1,0:T(8,128)S(1)} collective-permute-done((f32[2,128,128]{2,1,0:T(8,128)S(1)}, f32[2,128,128]{2,1,0:T(8,128)S(1)}, u32[]{:S(2)}, u32[]{:S(2)}) %collective-permute-start.7) | collective-permute-done | bytes 131104 | tf_op jit(solution)/shard_map/ppermute | solution.py:23
  49.2 1.8 %shard_map.82 = f32[128,8,128]{2,1,0:T(8,128)} custom-call(bf16[2,256,512]{2,1,0:T(8,128)(2,1)S(1)} %get-tuple-element.56.refs_0_, bf16[2,256,512]{2,1,0:T(8,128)(2,1)S(1)} %get-tuple-element.68.refs_1_, f32[4,256,128]{2,1,0:T(8,128)S(1)} %get-tuple-element.69.refs_2_, f32[4,256,128]{2,1,0:T(8,128)S(1)} %get-tuple-element.70.refs_3_, ...), custom_call_target="tpu_custom_call" | custom-call | tf_op jit(solution)/shard_map/pallas_call | solution.py:370
  51.0 1.0 %shard_map.85 = (f32[128,4,128]{2,1,0:T(4,128)}, f32[128,4,128]{2,1,0:T(4,128)}) custom-call(f32[2,128,128]{2,1,0:T(8,128)S(1)} %shard_map.83.refs_0_, f32[2,128,128]{2,1,0:T(8,128)S(1)} %shard_map.84.refs_1_, f32[2,128,128]{2,1,0:T(8,128)S(1)} %collective-permute-done.12.refs_2_, f32[2,128,128]{2,1,0:T(8,128)S(1)} %collective-permute-done.13.refs_3_), custom_call_target="tpu_custom_call" | custom-call | tf_op jit(solution)/shard_map/pallas_call | solution.py:370
  (14 shorter events, 0.2 us)
Async XLA Ops:
  1.9 13.4 %collective-permute-start.3 = (f32[2,128,128]{2,1,0:T(8,128)S(1)}, f32[2,128,128]{2,1,0:T(8,128)S(1)}, u32[]{:S(2)}, u32[]{:S(2)}) collective-permute-start(f32[2,128,128]{2,1,0:T(8,128)S(1)} %get-tuple-element.44.refs_4_.refs_9_), channel_id=1, source_target_pairs={{0,4},{4,8},{8,12},{1,5},{5,9},{9,13},{2,6},{6,10},{10,14},{3,7},{... | collective-permute-start | bytes 393224 | tf_op jit(solution)/shard_map/ppermute | solution.py:23
  6.8 14.4 %collective-permute-start.4 = (f32[2,128,128]{2,1,0:T(8,128)S(1)}, f32[2,128,128]{2,1,0:T(8,128)S(1)}, u32[]{:S(2)}, u32[]{:S(2)}) collective-permute-start(f32[2,128,128]{2,1,0:T(8,128)S(1)} %get-tuple-element.44.refs_4_.refs_9_), channel_id=1, source_target_pairs={{0,8},{4,12},{1,9},{5,13},{2,10},{6,14},{3,11},{7,15},{16,24},{20,... | collective-permute-start | bytes 393224 | tf_op jit(solution)/shard_map/ppermute | solution.py:23
  11.3 9.9 %collective-permute-start.5 = (f32[2,128,128]{2,1,0:T(8,128)S(1)}, f32[2,128,128]{2,1,0:T(8,128)S(1)}, u32[]{:S(2)}, u32[]{:S(2)}) collective-permute-start(f32[2,128,128]{2,1,0:T(8,128)S(1)} %get-tuple-element.44.refs_4_.refs_9_), channel_id=1, source_target_pairs={{0,12},{1,13},{2,14},{3,15},{16,28},{17,29},{18,30},{19,31}} | collective-permute-start | bytes 393224 | tf_op jit(solution)/shard_map/ppermute | solution.py:23
  12.6 12.8 %collective-permute-start = (f32[2,128,128]{2,1,0:T(8,128)S(1)}, f32[2,128,128]{2,1,0:T(8,128)S(1)}, u32[]{:S(2)}, u32[]{:S(2)}) collective-permute-start(f32[2,128,128]{2,1,0:T(8,128)S(1)} %get-tuple-element.43.refs_3_.refs_4_.refs_8_), channel_id=1, source_target_pairs={{0,4},{4,8},{8,12},{1,5},{5,9},{9,13},{2,6},{6,10},{10,14},{3,7},{... | collective-permute-start | bytes 393224 | tf_op jit(solution)/shard_map/ppermute | solution.py:23
  13.9 12.8 %collective-permute-start.1 = (f32[2,128,128]{2,1,0:T(8,128)S(1)}, f32[2,128,128]{2,1,0:T(8,128)S(1)}, u32[]{:S(2)}, u32[]{:S(2)}) collective-permute-start(f32[2,128,128]{2,1,0:T(8,128)S(1)} %get-tuple-element.43.refs_3_.refs_4_.refs_8_), channel_id=1, source_target_pairs={{0,8},{4,12},{1,9},{5,13},{2,10},{6,14},{3,11},{7,15},{16,24},{20,... | collective-permute-start | bytes 393224 | tf_op jit(solution)/shard_map/ppermute | solution.py:23
  15.3 11.5 %collective-permute-start.2 = (f32[2,128,128]{2,1,0:T(8,128)S(1)}, f32[2,128,128]{2,1,0:T(8,128)S(1)}, u32[]{:S(2)}, u32[]{:S(2)}) collective-permute-start(f32[2,128,128]{2,1,0:T(8,128)S(1)} %get-tuple-element.43.refs_3_.refs_4_.refs_8_), channel_id=1, source_target_pairs={{0,12},{1,13},{2,14},{3,15},{16,28},{17,29},{18,30},{19,31}} | collective-permute-start | bytes 393224 | tf_op jit(solution)/shard_map/ppermute | solution.py:23
  22.8 8.1 %collective-permute-start.9 = (f32[2,128,128]{2,1,0:T(8,128)S(1)}, f32[2,128,128]{2,1,0:T(8,128)S(1)}, u32[]{:S(2)}, u32[]{:S(2)}) collective-permute-start(f32[2,128,128]{2,1,0:T(8,128)S(1)} %get-tuple-element.78), channel_id=1, source_target_pairs={{4,0},{8,4},{12,8},{5,1},{9,5},{13,9},{6,2},{10,6},{14,10},{7,3},{... | collective-permute-start | bytes 393224 | tf_op jit(solution)/shard_map/ppermute | solution.py:23
  24.1 13.6 %collective-permute-start.10 = (f32[2,128,128]{2,1,0:T(8,128)S(1)}, f32[2,128,128]{2,1,0:T(8,128)S(1)}, u32[]{:S(2)}, u32[]{:S(2)}) collective-permute-start(f32[2,128,128]{2,1,0:T(8,128)S(1)} %get-tuple-element.79), channel_id=1, source_target_pairs={{8,0},{12,4},{9,1},{13,5},{10,2},{14,6},{11,3},{15,7},{24,16},{28,... | collective-permute-start | bytes 393224 | tf_op jit(solution)/shard_map/ppermute | solution.py:23
  25.5 12.3 %collective-permute-start.11 = (f32[2,128,128]{2,1,0:T(8,128)S(1)}, f32[2,128,128]{2,1,0:T(8,128)S(1)}, u32[]{:S(2)}, u32[]{:S(2)}) collective-permute-start(f32[2,128,128]{2,1,0:T(8,128)S(1)} %get-tuple-element.80), channel_id=1, source_target_pairs={{12,0},{13,1},{14,2},{15,3},{28,16},{29,17},{30,18},{31,19}} | collective-permute-start | bytes 393224 | tf_op jit(solution)/shard_map/ppermute | solution.py:23
  28.4 12.1 %collective-permute-start.6 = (f32[2,128,128]{2,1,0:T(8,128)S(1)}, f32[2,128,128]{2,1,0:T(8,128)S(1)}, u32[]{:S(2)}, u32[]{:S(2)}) collective-permute-start(f32[2,128,128]{2,1,0:T(8,128)S(1)} %get-tuple-element.74), channel_id=1, source_target_pairs={{4,0},{8,4},{12,8},{5,1},{9,5},{13,9},{6,2},{10,6},{14,10},{7,3},{... | collective-permute-start | bytes 393224 | tf_op jit(solution)/shard_map/ppermute | solution.py:23
  29.7 19.4 %collective-permute-start.7 = (f32[2,128,128]{2,1,0:T(8,128)S(1)}, f32[2,128,128]{2,1,0:T(8,128)S(1)}, u32[]{:S(2)}, u32[]{:S(2)}) collective-permute-start(f32[2,128,128]{2,1,0:T(8,128)S(1)} %get-tuple-element.75), channel_id=1, source_target_pairs={{8,0},{12,4},{9,1},{13,5},{10,2},{14,6},{11,3},{15,7},{24,16},{28,... | collective-permute-start | bytes 393224 | tf_op jit(solution)/shard_map/ppermute | solution.py:23
  31.0 18.1 %collective-permute-start.8 = (f32[2,128,128]{2,1,0:T(8,128)S(1)}, f32[2,128,128]{2,1,0:T(8,128)S(1)}, u32[]{:S(2)}, u32[]{:S(2)}) collective-permute-start(f32[2,128,128]{2,1,0:T(8,128)S(1)} %get-tuple-element.76), channel_id=1, source_target_pairs={{12,0},{13,1},{14,2},{15,3},{28,16},{29,17},{30,18},{31,19}} | collective-permute-start | bytes 393224 | tf_op jit(solution)/shard_map/ppermute | solution.py:23
  37.8 13.2 %collective-permute-start.13 = (f32[2,128,128]{2,1,0:T(8,128)S(1)}, f32[2,128,128]{2,1,0:T(8,128)S(1)}, u32[]{:S(2)}, u32[]{:S(2)}) collective-permute-start(f32[2,128,128]{2,1,0:T(8,128)S(1)} %shard_map.84.refs_1_), channel_id=1, source_target_pairs={{0,1},{1,0},{2,3},{3,2},{4,5},{5,4},{6,7},{7,6},{8,9},{9,8},{10,11... | collective-permute-start | bytes 393224 | tf_op jit(solution)/shard_map/ppermute | solution.py:469
  49.1 1.9 %collective-permute-start.12 = (f32[2,128,128]{2,1,0:T(8,128)S(1)}, f32[2,128,128]{2,1,0:T(8,128)S(1)}, u32[]{:S(2)}, u32[]{:S(2)}) collective-permute-start(f32[2,128,128]{2,1,0:T(8,128)S(1)} %shard_map.83.refs_0_), channel_id=1, source_target_pairs={{0,1},{1,0},{2,3},{3,2},{4,5},{5,4},{6,7},{7,6},{8,9},{9,8},{10,11... | collective-permute-start | bytes 393224 | tf_op jit(solution)/shard_map/ppermute | solution.py:469

commit v2 on v0

v2 whole, which is shorter than its diff:
```python
import functools
import math

import jax
import jax.numpy as jnp
from jax import lax
from jax.experimental import pallas as pl
from jax.experimental.pallas import tpu as pltpu
from jax.sharding import PartitionSpec as P


NEG = -1e30
F32 = jnp.float32
BF16 = jnp.bfloat16

NT = (((1,), (1,)), ((), ()))
NN = (((1,), (0,)), ((), ()))


def along(value, pairs):
    return lax.ppermute(value, "ctx", pairs)


def split2(x):
    hi = x.astype(BF16)
    return hi, (x - hi.astype(F32)).astype(BF16)


def split3(x):
    hi = x.astype(BF16)
    rest = x - hi.astype(F32)
    mid = rest.astype(BF16)
    return hi, mid, (rest - mid.astype(F32)).astype(BF16)


def lanes(*parts):
    return jnp.concatenate(parts, axis=1)


def stack(*parts):
    return jnp.concatenate(parts, axis=0)


def dot(a, b, dims):
    return lax.dot_general(a, b, dims, preferred_element_type=F32)


def short3(a, b, dims):
    join = lanes if dims is NT else stack
    return dot(lanes(a[0], a[0], a[1]), join(b[0], b[1], b[0]), dims)


def short6(a, b, dims):
    join = lanes if dims is NT else stack
    return dot(
        lanes(a[1], a[2], a[0], a[1], a[0], a[0]),
        join(b[1], b[0], b[2], b[0], b[1], b[0]),
        dims,
    )


def tall3(a, b, dims):
    m = a[0].shape[0]
    both = dot(stack(a[0], a[1]), b[0], dims)
    return both[:m] + (both[m:] + dot(a[0], b[1], dims))


def wide3(a, b, dims):
    if dims is NT:
        n = b[0].shape[0]
        both = dot(a[0], stack(b[0], b[1]), dims)
    else:
        n = b[0].shape[1]
        both = dot(a[0], lanes(b[0], b[1]), dims)
    return both[:, :n] + (both[:, n:] + dot(a[1], b[0], dims))


def colsum(x):
    return jnp.sum(x, axis=0, keepdims=True)


def colmax(x):
    return jnp.max(x, axis=0, keepdims=True)


def softmax_pair(mapped):
    up = jnp.exp(mapped - colmax(mapped))
    low = jnp.exp(jnp.min(mapped, axis=0, keepdims=True) - mapped)
    return stack(up * (1.0 / colsum(up)), low * (1.0 / colsum(low)))


def softmax_pair_back(feat, grad, width):
    up, low = feat[:width], feat[width:]
    gup, glow = grad[:width], grad[width:]
    return up * (gup - colsum(up * gup)) - low * (glow - colsum(low * glow))


def pack_kernel(cfg, *refs):
    sources, kv_refs = refs[:5], refs[5 : 5 + cfg.groups]
    q_ref, wq_ref, wk_ref, up_ref, k_ref, v_ref, sems = refs[5 + cfg.groups :]
    copies = [
        pltpu.make_async_copy(src, dst, sems.at[i])
        for i, (src, dst) in enumerate(zip(sources, (k_ref, v_ref, q_ref, wq_ref, wk_ref)))
    ]
    for copy in copies:
        copy.start()
    sub = lax.axis_index("sub")
    for slot, ref in enumerate((k_ref, v_ref)):
        copies[slot].wait()
        for g, kv_ref in enumerate(kv_refs):
            value = ref[:, cfg.starts[0] + g, :]
            for s in range(1, len(cfg.starts)):
                value = jnp.where(sub == s, ref[:, cfg.starts[s] + g, :], value)
            kv_ref[slot] = value
            if g == 0:
                up_ref[slot] = value
    copies[2].wait()
    for h in range(cfg.per_group):
        up_ref[2 + h] = q_ref[:, h, :]
    for copy in copies[3:]:
        copy.wait()


def prep_kernel(cfg, g, moved, *refs):
    if moved:
        up_ref, wq_ref, *outs = refs

        @pl.when(lax.axis_index("ctx") == cfg.helper)
        def _():
            rows = [up_ref[2 + h] for h in range(cfg.per_group)]
            prepare_rows(cfg, g, rows, up_ref, wq_ref, outs)

        return
    q_ref, wq_ref, wk_ref, own_ref, *outs = refs
    width, per_group = cfg.width, cfg.per_group
    rows = [q_ref[:, g * per_group + h, :] for h in range(per_group)]
    prepare_rows(cfg, g, rows, own_ref, wq_ref, outs[:6])
    wk_out, wk2_out, wq2_out = outs[6:]
    for h in range(per_group):
        part = split3(wk_ref[g * per_group + h].T)
        for i in range(3):
            wk_out[h * width : (h + 1) * width, i * width : (i + 1) * width] = part[i]
        for out, ref in ((wk2_out, wk_ref), (wq2_out, wq_ref)):
            part = split2(ref[g * per_group + h])
            for i in range(2):
                at = i * per_group + h
                out[:, at * width : (at + 1) * width] = part[i]


def prepare_rows(cfg, g, blocks, own_ref, wq_ref, outs):
    tokens, width, per_group = cfg.tokens, cfg.width, cfg.per_group
    rows = per_group * tokens
    scale = 1.0 / math.sqrt(width)
    key_row = lax.broadcasted_iota(jnp.int32, (tokens, rows), 0)
    query_col = lax.broadcasted_iota(jnp.int32, (tokens, rows), 1) % tokens
    q_out, fq_out, a_out, num_out, top_out, mass_out = outs
    query = split3(stack(*blocks))
    for i in range(3):
        q_out[:, i * width : (i + 1) * width] = query[i]
    scores = short6(split3(own_ref[0]), query, NT) * scale
    scores = jnp.where(key_row <= query_col, scores, NEG)
    top = colmax(scores)
    a = jnp.exp(scores - top)
    a_out[...] = a
    top_out[...] = top
    mass_out[...] = colsum(a)
    num_out[...] = short3(split2(own_ref[1].T), split2(a), NN)
    for h in range(per_group):
        piece = tuple(x[h * tokens : (h + 1) * tokens] for x in query)
        feat = split2(softmax_pair(short6(split3(wq_ref[g * per_group + h].T), piece, NT)))
        fq_out[h, :, :tokens] = feat[0]
        fq_out[h, :, tokens:] = feat[1]


def position_of(cfg, kind):
    here = lax.axis_index("ctx")
    if kind == "stay":
        return jnp.where(here == cfg.devices - 1, -1, here)
    if kind == "moved":
        return jnp.where(here == cfg.helper, cfg.devices - 1, -1)
    return here


def guarded(kernel):
    def body(cfg, kind, n, grads_at, *refs):
        here = position_of(cfg, kind)
        if kind == "all":
            kernel(cfg, n, here, *refs)
            return

        @pl.when(here >= 0)
        def _():
            kernel(cfg, n, here, *refs)

        @pl.when(here < 0)
        def _():
            for ref in refs[grads_at[0] : grads_at[1]]:
                ref[...] = jnp.zeros(ref.shape, F32)

    return body


@guarded
def attend_kernel(cfg, n, here, *refs):
    q_ref, fq_ref, a_ref, num_ref, top_ref, mass_ref, wk_t_ref, wk2_ref = refs[:8]
    kv_in = (None,) + refs[8 : 7 + n]
    win_ref, grad_ref, gden_ref, dfq_s = refs[7 + n : 11 + n]
    kv_out = (None, None) + refs[11 + n : 9 + 2 * n]
    (kv_s, dkv_s, top_s, mass_s, tnum_s, num_s, den_s, c_s, fk_s) = refs[9 + 2 * n :]
    tokens, width, per_group = cfg.tokens, cfg.width, cfg.per_group
    scale = 1.0 / math.sqrt(width)

    for k in range(2, n):
        pair, at = k // 2 - 1, (k % 2) * tokens
        for slot in range(2):
            kv_s[pair, slot, at : at + tokens, :] = kv_in[k][slot]
    query = tuple(q_ref[:, i * width : (i + 1) * width] for i in range(3))

    def head(x, h):
        return x[:, h * tokens : (h + 1) * tokens]

    def fq(h):
        return fq_ref[h, :, :tokens], fq_ref[h, :, tokens:]

    key_prev, value_prev = kv_in[1][0], kv_in[1][1]
    s_prev = short6(split3(key_prev), query, NT) * scale
    s_prev = jnp.where(here > 0, s_prev, NEG)
    top = jnp.maximum(top_ref[...], colmax(s_prev))
    a_prev = jnp.exp(s_prev - top)
    fade = jnp.exp(top_ref[...] - top)
    a_own = a_ref[...] * fade
    win_ref[:tokens] = a_own
    win_ref[tokens:] = a_prev
    mass = mass_ref[...] * fade + colsum(a_prev)
    wnum = num_ref[...] * fade + short3(
        split2(value_prev.T), split2(a_prev), NN
    )
    top_s[...] = top
    mass_s[...] = mass
    tnum_s[...] = wnum
    num_s[...] = wnum
    den_s[...] = mass

    def far_forward(pair, blocks):
        keys = blocks * tokens
        key, value = kv_s[pair, 0, :keys], kv_s[pair, 1, :keys]
        key_3 = split3(key)
        s = short6(key_3, query, NT) * scale
        old = top_s[...]
        new = jnp.maximum(old, colmax(s))
        p = jnp.exp(s - new)
        factor = jnp.exp(old - new)
        top_s[...] = new
        mass_s[...] = mass_s[...] * factor + colsum(p)
        wk_t = tuple(wk_t_ref[:, i * width : (i + 1) * width] for i in range(3))
        mapped = short6(wk_t, key_3, NT)
        for h in range(per_group):
            feat_t = softmax_pair(mapped[h * width : (h + 1) * width])
            fk_s[pair, h, :, :keys] = feat_t
            c_s[pair, :keys, h * tokens : (h + 1) * tokens] = wide3(
                split2(feat_t.T), fq(h), NN
            )
        c = c_s[pair, :keys]
        den_s[...] += colsum(c)
        value_t = split2(value.T)
        tnum_s[...] = tnum_s[...] * factor + tall3(value_t, split2(p), NN)
        num_s[...] += tall3(value_t, split2(c), NN)

    count = jnp.maximum(here - 1, 0)

    def over_far(body):
        def step(pair, carry):
            body(pair, 2)
            return carry

        if n > 3:
            lax.fori_loop(0, count // 2, step, 0)

        @pl.when(count % 2 == 1)
        def _():
            body(count // 2, 1)

    over_far(far_forward)

    inv = 1.0 / den_s[...]
    out = num_s[...] * inv
    residual = out - tnum_s[...] * (1.0 / mass_s[...])
    grad = residual * inv
    grad_2 = split2(grad)
    grad_ref[0] = grad_2[0]
    grad_ref[1] = grad_2[1]
    grad_den = -colsum(residual * out) * inv
    gden_ref[...] = grad_den
    dfq_s[...] = jnp.zeros_like(dfq_s)

    def far_backward(pair, blocks):
        keys = blocks * tokens
        dc = short3(split2(kv_s[pair, 1, :keys]), grad_2, NN) + grad_den
        dc_2 = split2(dc)
        dkv_s[pair, 1, :keys] = wide3(split2(c_s[pair, :keys]), grad_2, NT)
        pieces = []
        for h in range(per_group):
            feat_t = fk_s[pair, h, :, :keys]
            dc_h = tuple(head(x, h) for x in dc_2)
            dfq_s[h] += wide3(split2(feat_t), dc_h, NN)
            dfk = short3(fq(h), dc_h, NT)
            pieces.append(softmax_pair_back(feat_t, dfk, width))
        wk_2 = wk2_ref[:, : per_group * width], wk2_ref[:, per_group * width :]
        dkv_s[pair, 0, :keys] = tall3(wk_2, split2(stack(*pieces)), NN).T

    over_far(far_backward)
    for k in range(2, n):
        pair, at = k // 2 - 1, (k % 2) * tokens

        @pl.when(here >= k)
        def _():
            for slot in range(2):
                kv_out[k][slot] = dkv_s[pair, slot, at : at + tokens, :]

        @pl.when(here < k)
        def _():
            kv_out[k][...] = jnp.zeros((2, tokens, width), F32)


@guarded
def window_kernel(cfg, n, here, *refs):
    q_ref, win_ref, grad_ref, gden_ref, own_ref, prev_ref, soft_ref = refs[:7]
    outs = refs[7:]
    tokens, width = cfg.tokens, cfg.width
    scale = 1.0 / math.sqrt(width)
    grad_2 = grad_ref[0], grad_ref[1]
    win = win_ref[...]
    soft = short3(split2(stack(own_ref[1], prev_ref[1])), grad_2, NN) + gden_ref[...]
    soft_2 = split2(win * soft * scale)
    soft_ref[0] = soft_2[0]
    soft_ref[1] = soft_2[1]
    dk = wide3(soft_2, (q_ref[:, :width], q_ref[:, width : 2 * width]), NN)
    dv = wide3(split2(win), grad_2, NT)
    for k, out in enumerate(outs):
        out[0] = dk[k * tokens : (k + 1) * tokens]
        out[1] = dv[k * tokens : (k + 1) * tokens]


def query_rows(cfg, soft_ref, dfq_ref, fq_ref, wq2_ref, own_ref, prev_ref):
    tokens, width, per_group = cfg.tokens, cfg.width, cfg.per_group
    key_t = split2(stack(own_ref[0], prev_ref[0]).T)
    dq = tall3(key_t, (soft_ref[0], soft_ref[1]), NN)
    for h in range(per_group):
        feat = fq_ref[h, :, :tokens].astype(F32) + fq_ref[h, :, tokens:].astype(F32)
        back = softmax_pair_back(feat, dfq_ref[h], width)
        wq_2 = tuple(
            wq2_ref[:, (i * per_group + h) * width : (i * per_group + h + 1) * width]
            for i in range(2)
        )
        dq_h = dq[:, h * tokens : (h + 1) * tokens] + short3(wq_2, split2(back), NN)
        yield h, dq_h.T


def query_kernel(cfg, *refs):
    dq_ref = refs[-1]
    for g in range(cfg.groups):
        if cfg.moves and g == 0:
            here = lax.axis_index("ctx")

            @pl.when(here != cfg.devices - 1)
            def _():
                for h, value in query_rows(cfg, *refs[:6]):
                    dq_ref[:, h, :] = value

            @pl.when(here == cfg.devices - 1)
            def _():
                for h in range(cfg.per_group):
                    dq_ref[:, h, :] = refs[-2][2 + h]
        else:
            for h, value in query_rows(cfg, *refs[6 * g : 6 * g + 6]):
                dq_ref[:, g * cfg.per_group + h, :] = value


def moved_query_kernel(cfg, *refs):
    own_grad_ref, out_ref = refs[6], refs[7]

    @pl.when(lax.axis_index("ctx") == cfg.helper)
    def _():
        out_ref[:2] = own_grad_ref[...]
        for h, value in query_rows(cfg, *refs[:6]):
            out_ref[2 + h] = value

    @pl.when(lax.axis_index("ctx") != cfg.helper)
    def _():
        out_ref[...] = jnp.zeros(out_ref.shape, F32)


def add_kernel(*refs):
    total = refs[0][...]
    for ref in refs[1:-1]:
        total = total + ref[:2]
    refs[-1][...] = total


def place_kernel(cfg, *refs):
    sub = lax.axis_index("sub")
    mine, other = refs[: cfg.groups], refs[cfg.groups : 2 * cfg.groups]
    for slot, ref in enumerate(refs[2 * cfg.groups :]):
        for g in range(cfg.groups_dev):
            if cfg.shared:
                ref[:, g, :] = mine[g][slot] + other[g][slot]
            else:
                owner, at = g // cfg.groups, g % cfg.groups
                ref[:, g, :] = jnp.where(sub == owner, mine[at][slot], other[at][slot])


class Config:
    def __init__(self, queries, key_vectors):
        self.tokens, self.heads, self.width = queries.shape
        self.groups_dev = key_vectors.shape[1]
        self.devices = lax.axis_size("ctx")
        subs = lax.axis_size("sub")
        assert subs == 2
        size = self.heads * subs // self.groups_dev
        self.shared = self.heads < size
        self.groups = max(1, self.heads // size)
        self.per_group = self.heads // self.groups
        self.starts = [s * self.heads // size for s in range(subs)]
        if self.shared:
            assert self.groups_dev == 1
        assert self.devices % 2 == 0
        self.moves = self.devices == 4 and self.groups == 2
        self.helper = self.devices - 3


VMEM = pl.BlockSpec(memory_space=pltpu.VMEM)


def limit(mebibytes):
    return pltpu.CompilerParams(vmem_limit_bytes=mebibytes << 20)


def near(*arrays):
    return [pltpu.with_memory_space_constraint(x, pltpu.VMEM) for x in arrays]


def far_off(*arrays):
    return [pltpu.with_memory_space_constraint(x, pltpu.HBM) for x in arrays]


def call(kernel, outs, args, scratch=(), ins=None, megabytes=16):
    return pl.pallas_call(
        kernel,
        out_shape=outs,
        in_specs=ins or [VMEM] * len(args),
        out_specs=jax.tree.map(lambda _: VMEM, outs),
        scratch_shapes=scratch,
        compiler_params=limit(megabytes),
    )(*args)


def layer(queries, key_vectors, value_vectors, query_feature, key_feature):
    cfg = Config(queries, key_vectors)
    tokens, width, groups, per_group = cfg.tokens, cfg.width, cfg.groups, cfg.per_group
    n, rows = cfg.devices, cfg.per_group * cfg.tokens
    kv_shape = pltpu.VMEM((2, tokens, width), F32)
    up_shape = pltpu.VMEM((2 + per_group, tokens, width), F32)
    loaded = (queries, query_feature, key_feature)
    *own, q, wq, wk, up = call(
        functools.partial(pack_kernel, cfg),
        (kv_shape,) * groups + tuple(pltpu.VMEM(x.shape, F32) for x in loaded) + (up_shape,),
        far_off(key_vectors, value_vectors, *loaded),
        [
            pltpu.VMEM(key_vectors.shape, F32),
            pltpu.VMEM(value_vectors.shape, F32),
            pltpu.SemaphoreType.DMA((5,)),
        ],
        [pl.BlockSpec(memory_space=pl.ANY)] * 5,
    )

    row_shapes = (
        pltpu.VMEM((rows, 3 * width), BF16),
        pltpu.VMEM((per_group, 2 * width, 2 * tokens), BF16),
        pltpu.VMEM((tokens, rows), F32),
        pltpu.VMEM((width, rows), F32),
        pltpu.VMEM((1, rows), F32),
        pltpu.VMEM((1, rows), F32),
    )
    weight_shapes = (
        pltpu.VMEM((per_group * width, 3 * width), BF16),
        pltpu.VMEM((width, 2 * per_group * width), BF16),
        pltpu.VMEM((width, 2 * per_group * width), BF16),
    )
    attend_shapes = (
        pltpu.VMEM((2 * tokens, rows), F32),
        pltpu.VMEM((2, width, rows), BF16),
        pltpu.VMEM((1, rows), F32),
        pltpu.VMEM((per_group, 2 * width, tokens), F32),
    )
    soft_shape = pltpu.VMEM((2, 2 * tokens, rows), BF16)

    def task(kind, ready, weights, kv):
        count = len(kv)
        pairs = max(1, (count - 1) // 2)
        wk_t, wk_2, wq_2 = weights
        scratch = [
            pltpu.VMEM((pairs, 2, 2 * tokens, width), F32),
            pltpu.VMEM((pairs, 2, 2 * tokens, width), F32),
            pltpu.VMEM((1, rows), F32),
            pltpu.VMEM((1, rows), F32),
            pltpu.VMEM((width, rows), F32),
            pltpu.VMEM((width, rows), F32),
            pltpu.VMEM((1, rows), F32),
            pltpu.VMEM((pairs, 2 * tokens, rows), F32),
            pltpu.VMEM((pairs, per_group, 2 * width, 2 * tokens), F32),
        ]
        win, grad, gden, dfq, *grads = call(
            functools.partial(
                attend_kernel, cfg, kind, count, (11 + count, 9 + 2 * count)
            ),
            attend_shapes + (kv_shape,) * (count - 2),
            near(*ready, wk_t, wk_2, *kv[1:]),
            scratch,
            megabytes=20,
        )
        soft, *near_grads = call(
            functools.partial(window_kernel, cfg, kind, count, (7, 9)),
            (soft_shape, kv_shape, kv_shape),
            near(ready[0], win, grad, gden, kv[0], kv[1]),
        )
        return near_grads + grads, (soft, dfq, ready[1], wq_2, kv[0], kv[1])

    def add(*parts):
        return call(add_kernel, kv_shape, near(*parts))

    def down(k, limit=n):
        return [(i, i + k) for i in range(limit - k)]

    def back(k, limit=n):
        return [(i, i - k) for i in range(k, limit)]

    ready, weights, kv, moved_kv = [], [], [], None
    for g in range(groups):
        limit = n - 1 if cfg.moves and g == 0 else n
        kv.append([own[g]])
        for k in range(1, limit):
            kv[g].append(along(own[g], down(k, limit)))
        made = call(
            functools.partial(prep_kernel, cfg, g, False),
            row_shapes + weight_shapes,
            near(q, wq, wk, own[g]),
        )
        ready.append(made[:6])
        weights.append(made[6:])
    if cfg.moves:
        arrived = along(up, [(n - 1, cfg.helper)])
        above = along(own[0], [(n - 2, cfg.helper)])
        moved_ready = call(
            functools.partial(prep_kernel, cfg, 0, True), row_shapes, near(arrived, wq)
        )
        moved_kv = [arrived, above, kv[0][0], kv[0][1]]

    for_query, mine, extra = [], [], []
    for g in range(groups):
        stays = cfg.moves and g == 0
        grads, query_parts = task(
            "stay" if stays else "all", ready[g], weights[g], kv[g]
        )
        for_query.append(query_parts)
        if not stays:
            got = [along(grads[k], back(k)) for k in range(1, n)]
            mine.append(add(grads[0], *got))
            continue
        moved, moved_parts = task("moved", moved_ready, weights[0], moved_kv)
        answer = call(
            functools.partial(moved_query_kernel, cfg),
            up_shape,
            near(*moved_parts, moved[0]),
        )
        first = add(grads[1], moved[3])
        got = [
            along(grads[2], back(2, n - 1)),
            along(grads[1], [(n - 2, n - 3)]),
            along(first, [(cfg.helper, 0)]),
            along(moved[1], [(cfg.helper, n - 2)]),
            along(answer, [(cfg.helper, n - 1)]),
        ]
        extra = [got[-1]]
        mine.append(add(grads[0], moved[2], *got))
    query_grad = call(
        functools.partial(query_kernel, cfg),
        jax.ShapeDtypeStruct(queries.shape, F32),
        near(*[x for parts in for_query for x in parts], *extra),
    )
    other = [lax.ppermute(part, "sub", [(0, 1), (1, 0)]) for part in mine]
    key_grad, value_grad = call(
        functools.partial(place_kernel, cfg),
        (
            jax.ShapeDtypeStruct(key_vectors.shape, F32),
            jax.ShapeDtypeStruct(value_vectors.shape, F32),
        ),
        near(*mine, *other),
    )
    return query_grad, key_grad, value_grad


def solution(mesh):
    placed = (
        P(("groups", "ctx"), ("head", "sub"), None),
        P(("groups", "ctx"), "head", None),
        P(("groups", "ctx"), "head", None),
        P(("head", "sub"), None, None),
        P(("head", "sub"), None, None),
    )

    def step(queries, key_vectors, value_vectors, query_feature, key_feature):
        return jax.shard_map(
            layer,
            mesh=mesh,
            in_specs=placed,
            out_specs=placed[:3],
            check_vma=False,
        )(queries, key_vectors, value_vectors, query_feature, key_feature)

    return step
```

time: 54 us -> 61.1 us (1.13)
  starting transfers between devices: 23.4 us -> 30.1 us
  local copies, waits for them, and re-layouts: 4.03 us -> 0 us
  waiting for transfers between devices: 16.6 us -> 19 us
  Pallas kernels: 8.67 us -> 10.8 us
    ppermute x12 -> x15, starting transfers between devices: 23.2 us -> 30 us  [along(): return lax.ppermute(value, 'ctx', pairs)]
    unnamed x10 -> x0, local copies, waits for them, and re-layouts: 4.03 us -> none
    ppermute x12 -> x15, waiting for transfers between devices: 16.6 us -> 18.9 us  [along(): return lax.ppermute(value, 'ctx', pairs)]
    pallas_call x10 -> x16, Pallas kernels: 8.67 us -> 10.8 us  [call(): pl.pallas_call(kernel, out_shape=outs, in_specs=ins or [VMEM] * len(args)...]
  transfers between devices with their start and end apart: 14 -> 17, of which waited for: 3 -> 4; matrix products, arithmetic and copies ran while one was open for 0% -> 0% of each run, Pallas kernels for 14% -> 13%
where the time goes in v2:
time: 61.1 us; the launch traced here: 60.8 us
  starting transfers between devices  30.1 us (49%)
  waiting for transfers between devices  19 us (31%)
  Pallas kernels  10.8 us (18%)
  between operations  0.93 us (2%)
    ppermute x15, starting transfers between devices, along(): return lax.ppermute(value, 'ctx', pairs)  30 us
    ppermute x15, waiting for transfers between devices, along(): return lax.ppermute(value, 'ctx', pairs)  18.9 us
    pallas_call x16, Pallas kernels, call(): pl.pallas_call(kernel, out_shape=outs, in_specs=ins or [VMEM] * len(args)...  10.8 us
  transfers between devices with their start and end apart: 17, of which 4 were waited for; matrix products, arithmetic and copies ran while one was open for 0% of the time, Pallas kernels for 13%

profile of v2, /device:TPU:0, one launch (start us, length us, event | category | flops | bytes accessed | tf_op | source)
XLA Modules:
  0.0 60.8 jit_solution(17702905211733289129)
XLA Ops:
  0.6 1.6 %shard_map.76 = (f32[2,128,128]{2,1,0:T(8,128)S(1)}, f32[2,128,128]{2,1,0:T(8,128)S(1)}, f32[128,8,128]{2,1,0:T(8,128)S(1)}, f32[8,128,128]{2,1,0:T(8,128)S(1)},...) custom-call(f32[128,4,128]{2,1,0:T(4,128)} %refs_0_.1, f32[128,4,128]{2,1,0:T(4,128)} %refs_1_.1, ...), custom_call_target="tpu_custom_call" | custom-call | tf_op jit(solution)/shard_map/pallas_call | solution.py:447
  2.2 0.7 %collective-permute-start.5 = (f32[6,128,128]{2,1,0:T(8,128)S(1)}, f32[6,128,128]{2,1,0:T(8,128)S(1)}, u32[]{:S(2)}, u32[]{:S(2)}) collective-permute-start(f32[6,128,128]{2,1,0:T(8,128)S(1)} %get-tuple-element.94), channel_id=1, source_target_pairs={{12,4},{13,5},{14,6},{15,7},{28,20},{29,21},{30,22},{31,23}} | collective-permute-start | bytes 1179656 | tf_op jit(solution)/shard_map/ppermute | solution.py:21
  3.6 6.2 %collective-permute-start = (f32[2,128,128]{2,1,0:T(8,128)S(1)}, f32[2,128,128]{2,1,0:T(8,128)S(1)}, u32[]{:S(2)}, u32[]{:S(2)}) collective-permute-start(f32[2,128,128]{2,1,0:T(8,128)S(1)} %get-tuple-element.64.refs_3_.refs_4_.refs_9_), channel_id=1, source_target_pairs={{0,4},{4,8},{1,5},{5,9},{2,6},{6,10},{3,7},{7,11},{16,20},{20,24},... | collective-permute-start | bytes 393224 | tf_op jit(solution)/shard_map/ppermute | solution.py:21
  9.8 3.0 %collective-permute-start.4 = (f32[2,128,128]{2,1,0:T(8,128)S(1)}, f32[2,128,128]{2,1,0:T(8,128)S(1)}, u32[]{:S(2)}, u32[]{:S(2)}) collective-permute-start(f32[2,128,128]{2,1,0:T(8,128)S(1)} %get-tuple-element.79.refs_3_.refs_4_.refs_10_), channel_id=1, source_target_pairs={{0,12},{1,13},{2,14},{3,15},{16,28},{17,29},{18,30},{19,31}} | collective-permute-start | bytes 393224 | tf_op jit(solution)/shard_map/ppermute | solution.py:21
  12.8 1.3 %collective-permute-start.3 = (f32[2,128,128]{2,1,0:T(8,128)S(1)}, f32[2,128,128]{2,1,0:T(8,128)S(1)}, u32[]{:S(2)}, u32[]{:S(2)}) collective-permute-start(f32[2,128,128]{2,1,0:T(8,128)S(1)} %get-tuple-element.79.refs_3_.refs_4_.refs_10_), channel_id=1, source_target_pairs={{0,8},{4,12},{1,9},{5,13},{2,10},{6,14},{3,11},{7,15},{16,24},{20,... | collective-permute-start | bytes 393224 | tf_op jit(solution)/shard_map/ppermute | solution.py:21
  14.1 6.8 %collective-permute-start.2 = (f32[2,128,128]{2,1,0:T(8,128)S(1)}, f32[2,128,128]{2,1,0:T(8,128)S(1)}, u32[]{:S(2)}, u32[]{:S(2)}) collective-permute-start(f32[2,128,128]{2,1,0:T(8,128)S(1)} %get-tuple-element.79.refs_3_.refs_4_.refs_10_), channel_id=1, source_target_pairs={{0,4},{4,8},{8,12},{1,5},{5,9},{9,13},{2,6},{6,10},{10,14},{3,7},{... | collective-permute-start | bytes 393224 | tf_op jit(solution)/shard_map/ppermute | solution.py:21
  20.9 1.3 %shard_map.77 = (bf16[512,384]{1,0:T(8,128)(2,1)S(1)}, bf16[4,256,256]{2,1,0:T(8,128)(2,1)S(1)}, f32[128,512]{1,0:T(8,128)S(1)}, f32[128,512]{1,0:T(8,128)S(1)},...) custom-call(f32[128,8,128]{2,1,0:T(8,128)S(1)} %get-tuple-element.61, ...), custom_call_target="tpu_custom_call" | custom-call | tf_op jit(solution)/shard_map/pallas_call | solution.py:447
  22.4 0.7 %collective-permute-start.7 = (f32[6,128,128]{2,1,0:T(8,128)S(1)}, f32[6,128,128]{2,1,0:T(8,128)S(1)}, u32[]{:S(2)}, u32[]{:S(2)}) collective-permute-start(f32[6,128,128]{2,1,0:T(8,128)S(1)} %shard_map.86), channel_id=1, source_target_pairs={{4,12},{5,13},{6,14},{7,15},{20,28},{21,29},{22,30},{23,31}} | collective-permute-start | bytes 1179656 | tf_op jit(solution)/shard_map/ppermute | solution.py:21
  23.1 2.9 %collective-permute-start.1 = (f32[2,128,128]{2,1,0:T(8,128)S(1)}, f32[2,128,128]{2,1,0:T(8,128)S(1)}, u32[]{:S(2)}, u32[]{:S(2)}) collective-permute-start(f32[2,128,128]{2,1,0:T(8,128)S(1)} %get-tuple-element.64.refs_3_.refs_4_.refs_9_), channel_id=1, source_target_pairs={{0,8},{1,9},{2,10},{3,11},{16,24},{17,25},{18,26},{19,27}} | collective-permute-start | bytes 393224 | tf_op jit(solution)/shard_map/ppermute | solution.py:21
  26.0 1.3 %shard_map.80 = (bf16[512,384]{1,0:T(8,128)(2,1)S(1)}, bf16[4,256,256]{2,1,0:T(8,128)(2,1)S(1)}, f32[128,512]{1,0:T(8,128)S(1)}, f32[128,512]{1,0:T(8,128)S(1)},...) custom-call(f32[128,8,128]{2,1,0:T(8,128)S(1)} %get-tuple-element.61, ...), custom_call_target="tpu_custom_call" | custom-call | tf_op jit(solution)/shard_map/pallas_call | solution.py:447
  27.3 1.1 %shard_map.81 = (f32[256,512]{1,0:T(8,128)S(1)}, bf16[2,128,512]{2,1,0:T(8,128)(2,1)S(1)}, f32[1,512]{1,0:T(1,128)S(1)}, f32[4,256,128]{2,1,0:T(8,128)S(1)}, f32...) custom-call(bf16[512,384]{1,0:T(8,128)(2,1)S(1)} %get-tuple-element.80.refs_0_, ...), custom_call_target="tpu_custom_call" | custom-call | tf_op jit(solution)/shard_map/pallas_call | solution.py:447
  29.0 1.3 %collective-permute-start.12 = (f32[2,128,128]{2,1,0:T(8,128)S(1)}, f32[2,128,128]{2,1,0:T(8,128)S(1)}, u32[]{:S(2)}, u32[]{:S(2)}) collective-permute-start(f32[2,128,128]{2,1,0:T(8,128)S(1)} %get-tuple-element.114), channel_id=1, source_target_pairs={{4,0},{8,4},{12,8},{5,1},{9,5},{13,9},{6,2},{10,6},{14,10},{7,3},{... | collective-permute-start | bytes 393224 | tf_op jit(solution)/shard_map/ppermute | solution.py:21
  30.3 1.3 %collective-permute-start.13 = (f32[2,128,128]{2,1,0:T(8,128)S(1)}, f32[2,128,128]{2,1,0:T(8,128)S(1)}, u32[]{:S(2)}, u32[]{:S(2)}) collective-permute-start(f32[2,128,128]{2,1,0:T(8,128)S(1)} %get-tuple-element.115), channel_id=1, source_target_pairs={{8,0},{12,4},{9,1},{13,5},{10,2},{14,6},{11,3},{15,7},{24,16},{28,... | collective-permute-start | bytes 393224 | tf_op jit(solution)/shard_map/ppermute | solution.py:21
  31.6 1.3 %collective-permute-start.14 = (f32[2,128,128]{2,1,0:T(8,128)S(1)}, f32[2,128,128]{2,1,0:T(8,128)S(1)}, u32[]{:S(2)}, u32[]{:S(2)}) collective-permute-start(f32[2,128,128]{2,1,0:T(8,128)S(1)} %get-tuple-element.116), channel_id=1, source_target_pairs={{12,0},{13,1},{14,2},{15,3},{28,16},{29,17},{30,18},{31,19}} | collective-permute-start | bytes 393224 | tf_op jit(solution)/shard_map/ppermute | solution.py:21
  33.0 0.9 %shard_map.78 = (f32[256,512]{1,0:T(8,128)S(1)}, bf16[2,128,512]{2,1,0:T(8,128)(2,1)S(1)}, f32[1,512]{1,0:T(1,128)S(1)}, f32[4,256,128]{2,1,0:T(8,128)S(1)}, f32[2,128,128]{2,1,0:T(8,128)S(1)}) custom-call(bf16[512,384]{1,0:T(8,128)(2,1)S(1)} %get-tuple-element.65.refs_0_, bf16[4,256,256]{2,1,0:T(8,128)(2,1)S(1)} %get-tuple-element.66.refs_1_.refs_2_, ...), custom_call_target="tpu_custom_call" | custom-call | tf_op jit(solution)/shard_map/pallas_call | solution.py:447
  33.8 0.7 %shard_map.79 = (bf16[2,256,512]{2,1,0:T(8,128)(2,1)S(1)}, f32[2,128,128]{2,1,0:T(8,128)S(1)}, f32[2,128,128]{2,1,0:T(8,128)S(1)}) custom-call(bf16[512,384]{1,0:T(8,128)(2,1)S(1)} %get-tuple-element.65.refs_0_, f32[256,512]{1,0:T(8,128)S(1)} %get-tuple-element.73.refs_1_, bf16[2,128,512]{2,1,0:T(8,128)(2,1)S(1)} %get-tuple-element.74.refs_2_, ...), custom_call_target="tpu_custom_call" | custom-call | tf_op jit(solution)/shard_map/pallas_call | solution.py:447
  35.2 4.6 %collective-permute-done.12.refs_1_ = f32[2,128,128]{2,1,0:T(8,128)S(1)} collective-permute-done((f32[2,128,128]{2,1,0:T(8,128)S(1)}, f32[2,128,128]{2,1,0:T(8,128)S(1)}, u32[]{:S(2)}, u32[]{:S(2)}) %collective-permute-start.12) | collective-permute-done | bytes 131104 | tf_op jit(solution)/shard_map/ppermute | solution.py:21
  39.9 1.3 %collective-permute-start.8 = (f32[2,128,128]{2,1,0:T(8,128)S(1)}, f32[2,128,128]{2,1,0:T(8,128)S(1)}, u32[]{:S(2)}, u32[]{:S(2)}) collective-permute-start(f32[2,128,128]{2,1,0:T(8,128)S(1)} %get-tuple-element.109), channel_id=1, source_target_pairs={{8,0},{9,1},{10,2},{11,3},{24,16},{25,17},{26,18},{27,19}} | collective-permute-start | bytes 393224 | tf_op jit(solution)/shard_map/ppermute | solution.py:21
  41.1 8.9 %collective-permute-done.13.refs_2_ = f32[2,128,128]{2,1,0:T(8,128)S(1)} collective-permute-done((f32[2,128,128]{2,1,0:T(8,128)S(1)}, f32[2,128,128]{2,1,0:T(8,128)S(1)}, u32[]{:S(2)}, u32[]{:S(2)}) %collective-permute-start.13) | collective-permute-done | bytes 131104 | tf_op jit(solution)/shard_map/ppermute | solution.py:21
  50.7 1.3 %collective-permute-start.10 = (f32[2,128,128]{2,1,0:T(8,128)S(1)}, f32[2,128,128]{2,1,0:T(8,128)S(1)}, u32[]{:S(2)}, u32[]{:S(2)}) collective-permute-start(f32[2,128,128]{2,1,0:T(8,128)S(1)} %shard_map.88), channel_id=1, source_target_pairs={{4,0},{5,1},{6,2},{7,3},{20,16},{21,17},{22,18},{23,19}} | collective-permute-start | bytes 393224 | tf_op jit(solution)/shard_map/ppermute | solution.py:21
  52.1 1.6 %collective-permute-done.8.refs_2_ = f32[2,128,128]{2,1,0:T(8,128)S(1)} collective-permute-done((f32[2,128,128]{2,1,0:T(8,128)S(1)}, f32[2,128,128]{2,1,0:T(8,128)S(1)}, u32[]{:S(2)}, u32[]{:S(2)}) %collective-permute-start.8) | collective-permute-done | bytes 131104 | tf_op jit(solution)/shard_map/ppermute | solution.py:21
  53.7 3.9 %collective-permute-done.10.refs_4_ = f32[2,128,128]{2,1,0:T(8,128)S(1)} collective-permute-done((f32[2,128,128]{2,1,0:T(8,128)S(1)}, f32[2,128,128]{2,1,0:T(8,128)S(1)}, u32[]{:S(2)}, u32[]{:S(2)}) %collective-permute-start.10) | collective-permute-done | bytes 131104 | tf_op jit(solution)/shard_map/ppermute | solution.py:21
  57.7 2.0 %shard_map.87 = f32[128,8,128]{2,1,0:T(8,128)} custom-call(bf16[2,256,512]{2,1,0:T(8,128)(2,1)S(1)} %get-tuple-element.76.refs_0_, f32[4,256,128]{2,1,0:T(8,128)S(1)} %get-tuple-element.77.refs_1_, bf16[4,256,256]{2,1,0:T(8,128)(2,1)S(1)} %get-tuple-element.66.refs_1_.refs_2_, bf16[128,1024]{1,0:T(8,128)(2,1)S(1)} %get-tuple-element.78.refs_3_, ...), custom_call_target="tpu_custom_call" | custom-call | tf_op jit(solution)/shard_map/pallas_call | solution.py:447
  59.7 1.0 %shard_map.91 = (f32[128,4,128]{2,1,0:T(4,128)}, f32[128,4,128]{2,1,0:T(4,128)}) custom-call(f32[2,128,128]{2,1,0:T(8,128)S(1)} %shard_map.89.refs_0_, f32[2,128,128]{2,1,0:T(8,128)S(1)} %shard_map.90.refs_1_, f32[2,128,128]{2,1,0:T(8,128)S(1)} %collective-permute-done.15.refs_2_, f32[2,128,128]{2,1,0:T(8,128)S(1)} %collective-permute-done.16.refs_3_), custom_call_target="tpu_custom_call" | custom-call | tf_op jit(solution)/shard_map/pallas_call | solution.py:447
  (26 shorter events, 3.1 us)
Async XLA Ops:
  2.2 11.9 %collective-permute-start.5 = (f32[6,128,128]{2,1,0:T(8,128)S(1)}, f32[6,128,128]{2,1,0:T(8,128)S(1)}, u32[]{:S(2)}, u32[]{:S(2)}) collective-permute-start(f32[6,128,128]{2,1,0:T(8,128)S(1)} %get-tuple-element.94), channel_id=1, source_target_pairs={{12,4},{13,5},{14,6},{15,7},{28,20},{29,21},{30,22},{31,23}} | collective-permute-start | bytes 1179656 | tf_op jit(solution)/shard_map/ppermute | solution.py:21
  2.9 19.3 %collective-permute-start.6 = (f32[2,128,128]{2,1,0:T(8,128)S(1)}, f32[2,128,128]{2,1,0:T(8,128)S(1)}, u32[]{:S(2)}, u32[]{:S(2)}) collective-permute-start(f32[2,128,128]{2,1,0:T(8,128)S(1)} %get-tuple-element.64.refs_3_.refs_4_.refs_9_), channel_id=1, source_target_pairs={{8,4},{9,5},{10,6},{11,7},{24,20},{25,21},{26,22},{27,23}} | collective-permute-start | bytes 393224 | tf_op jit(solution)/shard_map/ppermute | solution.py:21
  3.6 18.7 %collective-permute-start = (f32[2,128,128]{2,1,0:T(8,128)S(1)}, f32[2,128,128]{2,1,0:T(8,128)S(1)}, u32[]{:S(2)}, u32[]{:S(2)}) collective-permute-start(f32[2,128,128]{2,1,0:T(8,128)S(1)} %get-tuple-element.64.refs_3_.refs_4_.refs_9_), channel_id=1, source_target_pairs={{0,4},{4,8},{1,5},{5,9},{2,6},{6,10},{3,7},{7,11},{16,20},{20,24},... | collective-permute-start | bytes 393224 | tf_op jit(solution)/shard_map/ppermute | solution.py:21
  9.8 17.5 %collective-permute-start.4 = (f32[2,128,128]{2,1,0:T(8,128)S(1)}, f32[2,128,128]{2,1,0:T(8,128)S(1)}, u32[]{:S(2)}, u32[]{:S(2)}) collective-permute-start(f32[2,128,128]{2,1,0:T(8,128)S(1)} %get-tuple-element.79.refs_3_.refs_4_.refs_10_), channel_id=1, source_target_pairs={{0,12},{1,13},{2,14},{3,15},{16,28},{17,29},{18,30},{19,31}} | collective-permute-start | bytes 393224 | tf_op jit(solution)/shard_map/ppermute | solution.py:21
  12.8 14.4 %collective-permute-start.3 = (f32[2,128,128]{2,1,0:T(8,128)S(1)}, f32[2,128,128]{2,1,0:T(8,128)S(1)}, u32[]{:S(2)}, u32[]{:S(2)}) collective-permute-start(f32[2,128,128]{2,1,0:T(8,128)S(1)} %get-tuple-element.79.refs_3_.refs_4_.refs_10_), channel_id=1, source_target_pairs={{0,8},{4,12},{1,9},{5,13},{2,10},{6,14},{3,11},{7,15},{16,24},{20,... | collective-permute-start | bytes 393224 | tf_op jit(solution)/shard_map/ppermute | solution.py:21
  14.1 13.1 %collective-permute-start.2 = (f32[2,128,128]{2,1,0:T(8,128)S(1)}, f32[2,128,128]{2,1,0:T(8,128)S(1)}, u32[]{:S(2)}, u32[]{:S(2)}) collective-permute-start(f32[2,128,128]{2,1,0:T(8,128)S(1)} %get-tuple-element.79.refs_3_.refs_4_.refs_10_), channel_id=1, source_target_pairs={{0,4},{4,8},{8,12},{1,5},{5,9},{9,13},{2,6},{6,10},{10,14},{3,7},{... | collective-permute-start | bytes 393224 | tf_op jit(solution)/shard_map/ppermute | solution.py:21
  22.4 35.2 %collective-permute-start.7 = (f32[6,128,128]{2,1,0:T(8,128)S(1)}, f32[6,128,128]{2,1,0:T(8,128)S(1)}, u32[]{:S(2)}, u32[]{:S(2)}) collective-permute-start(f32[6,128,128]{2,1,0:T(8,128)S(1)} %shard_map.86), channel_id=1, source_target_pairs={{4,12},{5,13},{6,14},{7,15},{20,28},{21,29},{22,30},{23,31}} | collective-permute-start | bytes 1179656 | tf_op jit(solution)/shard_map/ppermute | solution.py:21
  23.1 9.9 %collective-permute-start.1 = (f32[2,128,128]{2,1,0:T(8,128)S(1)}, f32[2,128,128]{2,1,0:T(8,128)S(1)}, u32[]{:S(2)}, u32[]{:S(2)}) collective-permute-start(f32[2,128,128]{2,1,0:T(8,128)S(1)} %get-tuple-element.64.refs_3_.refs_4_.refs_9_), channel_id=1, source_target_pairs={{0,8},{1,9},{2,10},{3,11},{16,24},{17,25},{18,26},{19,27}} | collective-permute-start | bytes 393224 | tf_op jit(solution)/shard_map/ppermute | solution.py:21
  29.0 10.8 %collective-permute-start.12 = (f32[2,128,128]{2,1,0:T(8,128)S(1)}, f32[2,128,128]{2,1,0:T(8,128)S(1)}, u32[]{:S(2)}, u32[]{:S(2)}) collective-permute-start(f32[2,128,128]{2,1,0:T(8,128)S(1)} %get-tuple-element.114), channel_id=1, source_target_pairs={{4,0},{8,4},{12,8},{5,1},{9,5},{13,9},{6,2},{10,6},{14,10},{7,3},{... | collective-permute-start | bytes 393224 | tf_op jit(solution)/shard_map/ppermute | solution.py:21
  30.3 19.7 %collective-permute-start.13 = (f32[2,128,128]{2,1,0:T(8,128)S(1)}, f32[2,128,128]{2,1,0:T(8,128)S(1)}, u32[]{:S(2)}, u32[]{:S(2)}) collective-permute-start(f32[2,128,128]{2,1,0:T(8,128)S(1)} %get-tuple-element.115), channel_id=1, source_target_pairs={{8,0},{12,4},{9,1},{13,5},{10,2},{14,6},{11,3},{15,7},{24,16},{28,... | collective-permute-start | bytes 393224 | tf_op jit(solution)/shard_map/ppermute | solution.py:21
  31.6 19.0 %collective-permute-start.14 = (f32[2,128,128]{2,1,0:T(8,128)S(1)}, f32[2,128,128]{2,1,0:T(8,128)S(1)}, u32[]{:S(2)}, u32[]{:S(2)}) collective-permute-start(f32[2,128,128]{2,1,0:T(8,128)S(1)} %get-tuple-element.116), channel_id=1, source_target_pairs={{12,0},{13,1},{14,2},{15,3},{28,16},{29,17},{30,18},{31,19}} | collective-permute-start | bytes 393224 | tf_op jit(solution)/shard_map/ppermute | solution.py:21
  34.5 17.5 %collective-permute-start.9 = (f32[2,128,128]{2,1,0:T(8,128)S(1)}, f32[2,128,128]{2,1,0:T(8,128)S(1)}, u32[]{:S(2)}, u32[]{:S(2)}) collective-permute-start(f32[2,128,128]{2,1,0:T(8,128)S(1)} %get-tuple-element.110.refs_0_), channel_id=1, source_target_pairs={{8,4},{9,5},{10,6},{11,7},{24,20},{25,21},{26,22},{27,23}} | collective-permute-start | bytes 393224 | tf_op jit(solution)/shard_map/ppermute | solution.py:21
  39.9 13.8 %collective-permute-start.8 = (f32[2,128,128]{2,1,0:T(8,128)S(1)}, f32[2,128,128]{2,1,0:T(8,128)S(1)}, u32[]{:S(2)}, u32[]{:S(2)}) collective-permute-start(f32[2,128,128]{2,1,0:T(8,128)S(1)} %get-tuple-element.109), channel_id=1, source_target_pairs={{8,0},{9,1},{10,2},{11,3},{24,16},{25,17},{26,18},{27,19}} | collective-permute-start | bytes 393224 | tf_op jit(solution)/shard_map/ppermute | solution.py:21
  50.0 3.7 %collective-permute-start.11 = (f32[2,128,128]{2,1,0:T(8,128)S(1)}, f32[2,128,128]{2,1,0:T(8,128)S(1)}, u32[]{:S(2)}, u32[]{:S(2)}) collective-permute-start(f32[2,128,128]{2,1,0:T(8,128)S(1)} %get-tuple-element.112), channel_id=1, source_target_pairs={{4,8},{5,9},{6,10},{7,11},{20,24},{21,25},{22,26},{23,27}} | collective-permute-start | bytes 393224 | tf_op jit(solution)/shard_map/ppermute | solution.py:21
  50.7 6.9 %collective-permute-start.10 = (f32[2,128,128]{2,1,0:T(8,128)S(1)}, f32[2,128,128]{2,1,0:T(8,128)S(1)}, u32[]{:S(2)}, u32[]{:S(2)}) collective-permute-start(f32[2,128,128]{2,1,0:T(8,128)S(1)} %shard_map.88), channel_id=1, source_target_pairs={{4,0},{5,1},{6,2},{7,3},{20,16},{21,17},{22,18},{23,19}} | collective-permute-start | bytes 393224 | tf_op jit(solution)/shard_map/ppermute | solution.py:21
  52.0 7.7 %collective-permute-start.16 = (f32[2,128,128]{2,1,0:T(8,128)S(1)}, f32[2,128,128]{2,1,0:T(8,128)S(1)}, u32[]{:S(2)}, u32[]{:S(2)}) collective-permute-start(f32[2,128,128]{2,1,0:T(8,128)S(1)} %shard_map.90.refs_1_), channel_id=1, source_target_pairs={{0,1},{1,0},{2,3},{3,2},{4,5},{5,4},{6,7},{7,6},{8,9},{9,8},{10,11... | collective-permute-start | bytes 393224 | tf_op jit(solution)/shard_map/ppermute | solution.py:590
  57.6 2.1 %collective-permute-start.15 = (f32[2,128,128]{2,1,0:T(8,128)S(1)}, f32[2,128,128]{2,1,0:T(8,128)S(1)}, u32[]{:S(2)}, u32[]{:S(2)}) collective-permute-start(f32[2,128,128]{2,1,0:T(8,128)S(1)} %shard_map.89.refs_0_), channel_id=1, source_target_pairs={{0,1},{1,0},{2,3},{3,2},{4,5},{5,4},{6,7},{7,6},{8,9},{9,8},{10,11... | collective-permute-start | bytes 393224 | tf_op jit(solution)/shard_map/ppermute | solution.py:590

commit v3 on v2

--- a/solution.py
+++ b/solution.py
@@ -563,7 +563,13 @@
         )
         for_query.append(query_parts)
         if not stays:
-            got = [along(grads[k], back(k)) for k in range(1, n)]
+            got = []
+            for k in range(1, n):
+                routes = [back(k)]
+                if cfg.moves and k == 2:
+                    routes = [[pair] for pair in back(k)]
+                for route in routes:
+                    got.append(along(grads[k], route))
             mine.append(add(grads[0], *got))
             continue
         moved, moved_parts = task("moved", moved_ready, weights[0], moved_kv)

time: 61.1 us -> 60.6 us (level)
  starting transfers between devices: 30.1 us -> 29.3 us
    ppermute x15 -> x16, starting transfers between devices: 30 us -> 29.2 us  [along(): return lax.ppermute(value, 'ctx', pairs)]
    ppermute x15 -> x16, waiting for transfers between devices: 18.9 us -> 19.2 us  [along(): return lax.ppermute(value, 'ctx', pairs)]
  transfers between devices with their start and end apart: 17 -> 18, of which waited for: 4 -> 5; matrix products, arithmetic and copies ran while one was open for 0% -> 0% of each run, Pallas kernels for 13% -> 14%
where the time goes in v3:
time: 60.6 us; the launch traced here: 60.3 us
  starting transfers between devices  29.3 us (48%)
  waiting for transfers between devices  19.2 us (32%)
  Pallas kernels  10.8 us (18%)
  between operations  0.94 us (2%)
    ppermute x16, starting transfers between devices, along(): return lax.ppermute(value, 'ctx', pairs)  29.2 us
    ppermute x16, waiting for transfers between devices, along(): return lax.ppermute(value, 'ctx', pairs)  19.2 us
    pallas_call x16, Pallas kernels, call(): pl.pallas_call(kernel, out_shape=outs, in_specs=ins or [VMEM] * len(args)...  10.8 us
  transfers between devices with their start and end apart: 18, of which 5 were waited for; matrix products, arithmetic and copies ran while one was open for 0% of the time, Pallas kernels for 14%

profile of v3, /device:TPU:0, one launch (start us, length us, event | category | flops | bytes accessed | tf_op | source)
XLA Modules:
  0.0 60.3 jit_solution(8394601451063381591)
XLA Ops:
  0.6 1.6 %shard_map.76 = (f32[2,128,128]{2,1,0:T(8,128)S(1)}, f32[2,128,128]{2,1,0:T(8,128)S(1)}, f32[128,8,128]{2,1,0:T(8,128)S(1)}, f32[8,128,128]{2,1,0:T(8,128)S(1)},...) custom-call(f32[128,4,128]{2,1,0:T(4,128)} %refs_0_.1, f32[128,4,128]{2,1,0:T(4,128)} %refs_1_.1, ...), custom_call_target="tpu_custom_call" | custom-call | tf_op jit(solution)/shard_map/pallas_call | solution.py:447
  2.2 0.7 %collective-permute-start.5 = (f32[6,128,128]{2,1,0:T(8,128)S(1)}, f32[6,128,128]{2,1,0:T(8,128)S(1)}, u32[]{:S(2)}, u32[]{:S(2)}) collective-permute-start(f32[6,128,128]{2,1,0:T(8,128)S(1)} %get-tuple-element.94), channel_id=1, source_target_pairs={{12,4},{13,5},{14,6},{15,7},{28,20},{29,21},{30,22},{31,23}} | collective-permute-start | bytes 1179656 | tf_op jit(solution)/shard_map/ppermute | solution.py:21
  3.6 6.2 %collective-permute-start = (f32[2,128,128]{2,1,0:T(8,128)S(1)}, f32[2,128,128]{2,1,0:T(8,128)S(1)}, u32[]{:S(2)}, u32[]{:S(2)}) collective-permute-start(f32[2,128,128]{2,1,0:T(8,128)S(1)} %get-tuple-element.64.refs_3_.refs_4_.refs_9_), channel_id=1, source_target_pairs={{0,4},{4,8},{1,5},{5,9},{2,6},{6,10},{3,7},{7,11},{16,20},{20,24},... | collective-permute-start | bytes 393224 | tf_op jit(solution)/shard_map/ppermute | solution.py:21
  9.8 3.0 %collective-permute-start.4 = (f32[2,128,128]{2,1,0:T(8,128)S(1)}, f32[2,128,128]{2,1,0:T(8,128)S(1)}, u32[]{:S(2)}, u32[]{:S(2)}) collective-permute-start(f32[2,128,128]{2,1,0:T(8,128)S(1)} %get-tuple-element.79.refs_3_.refs_4_.refs_10_), channel_id=1, source_target_pairs={{0,12},{1,13},{2,14},{3,15},{16,28},{17,29},{18,30},{19,31}} | collective-permute-start | bytes 393224 | tf_op jit(solution)/shard_map/ppermute | solution.py:21
  12.8 1.3 %collective-permute-start.3 = (f32[2,128,128]{2,1,0:T(8,128)S(1)}, f32[2,128,128]{2,1,0:T(8,128)S(1)}, u32[]{:S(2)}, u32[]{:S(2)}) collective-permute-start(f32[2,128,128]{2,1,0:T(8,128)S(1)} %get-tuple-element.79.refs_3_.refs_4_.refs_10_), channel_id=1, source_target_pairs={{0,8},{4,12},{1,9},{5,13},{2,10},{6,14},{3,11},{7,15},{16,24},{20,... | collective-permute-start | bytes 393224 | tf_op jit(solution)/shard_map/ppermute | solution.py:21
  14.1 6.8 %collective-permute-start.2 = (f32[2,128,128]{2,1,0:T(8,128)S(1)}, f32[2,128,128]{2,1,0:T(8,128)S(1)}, u32[]{:S(2)}, u32[]{:S(2)}) collective-permute-start(f32[2,128,128]{2,1,0:T(8,128)S(1)} %get-tuple-element.79.refs_3_.refs_4_.refs_10_), channel_id=1, source_target_pairs={{0,4},{4,8},{8,12},{1,5},{5,9},{9,13},{2,6},{6,10},{10,14},{3,7},{... | collective-permute-start | bytes 393224 | tf_op jit(solution)/shard_map/ppermute | solution.py:21
  20.9 1.3 %shard_map.77 = (bf16[512,384]{1,0:T(8,128)(2,1)S(1)}, bf16[4,256,256]{2,1,0:T(8,128)(2,1)S(1)}, f32[128,512]{1,0:T(8,128)S(1)}, f32[128,512]{1,0:T(8,128)S(1)},...) custom-call(f32[128,8,128]{2,1,0:T(8,128)S(1)} %get-tuple-element.61, ...), custom_call_target="tpu_custom_call" | custom-call | tf_op jit(solution)/shard_map/pallas_call | solution.py:447
  22.2 1.4 %collective-permute-start.1 = (f32[2,128,128]{2,1,0:T(8,128)S(1)}, f32[2,128,128]{2,1,0:T(8,128)S(1)}, u32[]{:S(2)}, u32[]{:S(2)}) collective-permute-start(f32[2,128,128]{2,1,0:T(8,128)S(1)} %get-tuple-element.64.refs_3_.refs_4_.refs_9_), channel_id=1, source_target_pairs={{0,8},{1,9},{2,10},{3,11},{16,24},{17,25},{18,26},{19,27}} | collective-permute-start | bytes 393224 | tf_op jit(solution)/shard_map/ppermute | solution.py:21
  24.5 1.3 %shard_map.80 = (bf16[512,384]{1,0:T(8,128)(2,1)S(1)}, bf16[4,256,256]{2,1,0:T(8,128)(2,1)S(1)}, f32[128,512]{1,0:T(8,128)S(1)}, f32[128,512]{1,0:T(8,128)S(1)},...) custom-call(f32[128,8,128]{2,1,0:T(8,128)S(1)} %get-tuple-element.61, ...), custom_call_target="tpu_custom_call" | custom-call | tf_op jit(solution)/shard_map/pallas_call | solution.py:447
  25.8 1.1 %shard_map.81 = (f32[256,512]{1,0:T(8,128)S(1)}, bf16[2,128,512]{2,1,0:T(8,128)(2,1)S(1)}, f32[1,512]{1,0:T(1,128)S(1)}, f32[4,256,128]{2,1,0:T(8,128)S(1)}, f32...) custom-call(bf16[512,384]{1,0:T(8,128)(2,1)S(1)} %get-tuple-element.80.refs_0_, ...), custom_call_target="tpu_custom_call" | custom-call | tf_op jit(solution)/shard_map/pallas_call | solution.py:447
  27.6 1.3 %collective-permute-start.12 = (f32[2,128,128]{2,1,0:T(8,128)S(1)}, f32[2,128,128]{2,1,0:T(8,128)S(1)}, u32[]{:S(2)}, u32[]{:S(2)}) collective-permute-start(f32[2,128,128]{2,1,0:T(8,128)S(1)} %get-tuple-element.114), channel_id=1, source_target_pairs={{4,0},{8,4},{12,8},{5,1},{9,5},{13,9},{6,2},{10,6},{14,10},{7,3},{... | collective-permute-start | bytes 393224 | tf_op jit(solution)/shard_map/ppermute | solution.py:21
  28.9 1.3 %collective-permute-start.15 = (f32[2,128,128]{2,1,0:T(8,128)S(1)}, f32[2,128,128]{2,1,0:T(8,128)S(1)}, u32[]{:S(2)}, u32[]{:S(2)}) collective-permute-start(f32[2,128,128]{2,1,0:T(8,128)S(1)} %get-tuple-element.116), channel_id=1, source_target_pairs={{12,0},{13,1},{14,2},{15,3},{28,16},{29,17},{30,18},{31,19}} | collective-permute-start | bytes 393224 | tf_op jit(solution)/shard_map/ppermute | solution.py:21
  30.9 1.3 %collective-permute-start.13 = (f32[2,128,128]{2,1,0:T(8,128)S(1)}, f32[2,128,128]{2,1,0:T(8,128)S(1)}, u32[]{:S(2)}, u32[]{:S(2)}) collective-permute-start(f32[2,128,128]{2,1,0:T(8,128)S(1)} %get-tuple-element.115), channel_id=1, source_target_pairs={{8,0},{9,1},{10,2},{11,3},{24,16},{25,17},{26,18},{27,19}} | collective-permute-start | bytes 393224 | tf_op jit(solution)/shard_map/ppermute | solution.py:21
  32.2 0.9 %shard_map.78 = (f32[256,512]{1,0:T(8,128)S(1)}, bf16[2,128,512]{2,1,0:T(8,128)(2,1)S(1)}, f32[1,512]{1,0:T(1,128)S(1)}, f32[4,256,128]{2,1,0:T(8,128)S(1)}, f32[2,128,128]{2,1,0:T(8,128)S(1)}) custom-call(bf16[512,384]{1,0:T(8,128)(2,1)S(1)} %get-tuple-element.65.refs_0_, bf16[4,256,256]{2,1,0:T(8,128)(2,1)S(1)} %get-tuple-element.66.refs_1_.refs_2_, ...), custom_call_target="tpu_custom_call" | custom-call | tf_op jit(solution)/shard_map/pallas_call | solution.py:447
  33.1 0.7 %shard_map.79 = (bf16[2,256,512]{2,1,0:T(8,128)(2,1)S(1)}, f32[2,128,128]{2,1,0:T(8,128)S(1)}, f32[2,128,128]{2,1,0:T(8,128)S(1)}) custom-call(bf16[512,384]{1,0:T(8,128)(2,1)S(1)} %get-tuple-element.65.refs_0_, f32[256,512]{1,0:T(8,128)S(1)} %get-tuple-element.73.refs_1_, bf16[2,128,512]{2,1,0:T(8,128)(2,1)S(1)} %get-tuple-element.74.refs_2_, ...), custom_call_target="tpu_custom_call" | custom-call | tf_op jit(solution)/shard_map/pallas_call | solution.py:447
  33.8 5.0 %collective-permute-done.12.refs_1_ = f32[2,128,128]{2,1,0:T(8,128)S(1)} collective-permute-done((f32[2,128,128]{2,1,0:T(8,128)S(1)}, f32[2,128,128]{2,1,0:T(8,128)S(1)}, u32[]{:S(2)}, u32[]{:S(2)}) %collective-permute-start.12) | collective-permute-done | bytes 131104 | tf_op jit(solution)/shard_map/ppermute | solution.py:21
  39.4 6.1 %collective-permute-done.15.refs_4_ = f32[2,128,128]{2,1,0:T(8,128)S(1)} collective-permute-done((f32[2,128,128]{2,1,0:T(8,128)S(1)}, f32[2,128,128]{2,1,0:T(8,128)S(1)}, u32[]{:S(2)}, u32[]{:S(2)}) %collective-permute-start.15) | collective-permute-done | bytes 131104 | tf_op jit(solution)/shard_map/ppermute | solution.py:21
  45.5 1.3 %collective-permute-start.8 = (f32[2,128,128]{2,1,0:T(8,128)S(1)}, f32[2,128,128]{2,1,0:T(8,128)S(1)}, u32[]{:S(2)}, u32[]{:S(2)}) collective-permute-start(f32[2,128,128]{2,1,0:T(8,128)S(1)} %get-tuple-element.109), channel_id=1, source_target_pairs={{8,0},{9,1},{10,2},{11,3},{24,16},{25,17},{26,18},{27,19}} | collective-permute-start | bytes 393224 | tf_op jit(solution)/shard_map/ppermute | solution.py:21
  47.5 1.5 %collective-permute-done.13.refs_2_ = f32[2,128,128]{2,1,0:T(8,128)S(1)} collective-permute-done((f32[2,128,128]{2,1,0:T(8,128)S(1)}, f32[2,128,128]{2,1,0:T(8,128)S(1)}, u32[]{:S(2)}, u32[]{:S(2)}) %collective-permute-start.13) | collective-permute-done | bytes 131104 | tf_op jit(solution)/shard_map/ppermute | solution.py:21
  49.0 1.3 %collective-permute-start.10 = (f32[2,128,128]{2,1,0:T(8,128)S(1)}, f32[2,128,128]{2,1,0:T(8,128)S(1)}, u32[]{:S(2)}, u32[]{:S(2)}) collective-permute-start(f32[2,128,128]{2,1,0:T(8,128)S(1)} %shard_map.88), channel_id=1, source_target_pairs={{4,0},{5,1},{6,2},{7,3},{20,16},{21,17},{22,18},{23,19}} | collective-permute-start | bytes 393224 | tf_op jit(solution)/shard_map/ppermute | solution.py:21
  50.4 4.0 %collective-permute-done.8.refs_2_ = f32[2,128,128]{2,1,0:T(8,128)S(1)} collective-permute-done((f32[2,128,128]{2,1,0:T(8,128)S(1)}, f32[2,128,128]{2,1,0:T(8,128)S(1)}, u32[]{:S(2)}, u32[]{:S(2)}) %collective-permute-start.8) | collective-permute-done | bytes 131104 | tf_op jit(solution)/shard_map/ppermute | solution.py:21
  54.3 2.7 %collective-permute-done.10.refs_4_ = f32[2,128,128]{2,1,0:T(8,128)S(1)} collective-permute-done((f32[2,128,128]{2,1,0:T(8,128)S(1)}, f32[2,128,128]{2,1,0:T(8,128)S(1)}, u32[]{:S(2)}, u32[]{:S(2)}) %collective-permute-start.10) | collective-permute-done | bytes 131104 | tf_op jit(solution)/shard_map/ppermute | solution.py:21
  57.2 2.0 %shard_map.87 = f32[128,8,128]{2,1,0:T(8,128)} custom-call(bf16[2,256,512]{2,1,0:T(8,128)(2,1)S(1)} %get-tuple-element.76.refs_0_, f32[4,256,128]{2,1,0:T(8,128)S(1)} %get-tuple-element.77.refs_1_, bf16[4,256,256]{2,1,0:T(8,128)(2,1)S(1)} %get-tuple-element.66.refs_1_.refs_2_, bf16[128,1024]{1,0:T(8,128)(2,1)S(1)} %get-tuple-element.78.refs_3_, ...), custom_call_target="tpu_custom_call" | custom-call | tf_op jit(solution)/shard_map/pallas_call | solution.py:447
  59.2 1.0 %shard_map.91 = (f32[128,4,128]{2,1,0:T(4,128)}, f32[128,4,128]{2,1,0:T(4,128)}) custom-call(f32[2,128,128]{2,1,0:T(8,128)S(1)} %shard_map.89.refs_0_, f32[2,128,128]{2,1,0:T(8,128)S(1)} %shard_map.90.refs_1_, f32[2,128,128]{2,1,0:T(8,128)S(1)} %collective-permute-done.16.refs_2_, f32[2,128,128]{2,1,0:T(8,128)S(1)} %collective-permute-done.17.refs_3_), custom_call_target="tpu_custom_call" | custom-call | tf_op jit(solution)/shard_map/pallas_call | solution.py:447
  (28 shorter events, 4.5 us)
Async XLA Ops:
  2.2 11.9 %collective-permute-start.5 = (f32[6,128,128]{2,1,0:T(8,128)S(1)}, f32[6,128,128]{2,1,0:T(8,128)S(1)}, u32[]{:S(2)}, u32[]{:S(2)}) collective-permute-start(f32[6,128,128]{2,1,0:T(8,128)S(1)} %get-tuple-element.94), channel_id=1, source_target_pairs={{12,4},{13,5},{14,6},{15,7},{28,20},{29,21},{30,22},{31,23}} | collective-permute-start | bytes 1179656 | tf_op jit(solution)/shard_map/ppermute | solution.py:21
  2.9 19.3 %collective-permute-start.6 = (f32[2,128,128]{2,1,0:T(8,128)S(1)}, f32[2,128,128]{2,1,0:T(8,128)S(1)}, u32[]{:S(2)}, u32[]{:S(2)}) collective-permute-start(f32[2,128,128]{2,1,0:T(8,128)S(1)} %get-tuple-element.64.refs_3_.refs_4_.refs_9_), channel_id=1, source_target_pairs={{8,4},{9,5},{10,6},{11,7},{24,20},{25,21},{26,22},{27,23}} | collective-permute-start | bytes 393224 | tf_op jit(solution)/shard_map/ppermute | solution.py:21
  3.6 20.1 %collective-permute-start = (f32[2,128,128]{2,1,0:T(8,128)S(1)}, f32[2,128,128]{2,1,0:T(8,128)S(1)}, u32[]{:S(2)}, u32[]{:S(2)}) collective-permute-start(f32[2,128,128]{2,1,0:T(8,128)S(1)} %get-tuple-element.64.refs_3_.refs_4_.refs_9_), channel_id=1, source_target_pairs={{0,4},{4,8},{1,5},{5,9},{2,6},{6,10},{3,7},{7,11},{16,20},{20,24},... | collective-permute-start | bytes 393224 | tf_op jit(solution)/shard_map/ppermute | solution.py:21
  9.8 16.0 %collective-permute-start.4 = (f32[2,128,128]{2,1,0:T(8,128)S(1)}, f32[2,128,128]{2,1,0:T(8,128)S(1)}, u32[]{:S(2)}, u32[]{:S(2)}) collective-permute-start(f32[2,128,128]{2,1,0:T(8,128)S(1)} %get-tuple-element.79.refs_3_.refs_4_.refs_10_), channel_id=1, source_target_pairs={{0,12},{1,13},{2,14},{3,15},{16,28},{17,29},{18,30},{19,31}} | collective-permute-start | bytes 393224 | tf_op jit(solution)/shard_map/ppermute | solution.py:21
  12.8 13.0 %collective-permute-start.3 = (f32[2,128,128]{2,1,0:T(8,128)S(1)}, f32[2,128,128]{2,1,0:T(8,128)S(1)}, u32[]{:S(2)}, u32[]{:S(2)}) collective-permute-start(f32[2,128,128]{2,1,0:T(8,128)S(1)} %get-tuple-element.79.refs_3_.refs_4_.refs_10_), channel_id=1, source_target_pairs={{0,8},{4,12},{1,9},{5,13},{2,10},{6,14},{3,11},{7,15},{16,24},{20,... | collective-permute-start | bytes 393224 | tf_op jit(solution)/shard_map/ppermute | solution.py:21
  14.1 11.7 %collective-permute-start.2 = (f32[2,128,128]{2,1,0:T(8,128)S(1)}, f32[2,128,128]{2,1,0:T(8,128)S(1)}, u32[]{:S(2)}, u32[]{:S(2)}) collective-permute-start(f32[2,128,128]{2,1,0:T(8,128)S(1)} %get-tuple-element.79.refs_3_.refs_4_.refs_10_), channel_id=1, source_target_pairs={{0,4},{4,8},{8,12},{1,5},{5,9},{9,13},{2,6},{6,10},{10,14},{3,7},{... | collective-permute-start | bytes 393224 | tf_op jit(solution)/shard_map/ppermute | solution.py:21
  22.2 8.6 %collective-permute-start.1 = (f32[2,128,128]{2,1,0:T(8,128)S(1)}, f32[2,128,128]{2,1,0:T(8,128)S(1)}, u32[]{:S(2)}, u32[]{:S(2)}) collective-permute-start(f32[2,128,128]{2,1,0:T(8,128)S(1)} %get-tuple-element.64.refs_3_.refs_4_.refs_9_), channel_id=1, source_target_pairs={{0,8},{1,9},{2,10},{3,11},{16,24},{17,25},{18,26},{19,27}} | collective-permute-start | bytes 393224 | tf_op jit(solution)/shard_map/ppermute | solution.py:21
  23.8 33.3 %collective-permute-start.7 = (f32[6,128,128]{2,1,0:T(8,128)S(1)}, f32[6,128,128]{2,1,0:T(8,128)S(1)}, u32[]{:S(2)}, u32[]{:S(2)}) collective-permute-start(f32[6,128,128]{2,1,0:T(8,128)S(1)} %shard_map.86), channel_id=1, source_target_pairs={{4,12},{5,13},{6,14},{7,15},{20,28},{21,29},{22,30},{23,31}} | collective-permute-start | bytes 1179656 | tf_op jit(solution)/shard_map/ppermute | solution.py:21
  27.6 11.2 %collective-permute-start.12 = (f32[2,128,128]{2,1,0:T(8,128)S(1)}, f32[2,128,128]{2,1,0:T(8,128)S(1)}, u32[]{:S(2)}, u32[]{:S(2)}) collective-permute-start(f32[2,128,128]{2,1,0:T(8,128)S(1)} %get-tuple-element.114), channel_id=1, source_target_pairs={{4,0},{8,4},{12,8},{5,1},{9,5},{13,9},{6,2},{10,6},{14,10},{7,3},{... | collective-permute-start | bytes 393224 | tf_op jit(solution)/shard_map/ppermute | solution.py:21
  28.9 16.6 %collective-permute-start.15 = (f32[2,128,128]{2,1,0:T(8,128)S(1)}, f32[2,128,128]{2,1,0:T(8,128)S(1)}, u32[]{:S(2)}, u32[]{:S(2)}) collective-permute-start(f32[2,128,128]{2,1,0:T(8,128)S(1)} %get-tuple-element.116), channel_id=1, source_target_pairs={{12,0},{13,1},{14,2},{15,3},{28,16},{29,17},{30,18},{31,19}} | collective-permute-start | bytes 393224 | tf_op jit(solution)/shard_map/ppermute | solution.py:21
  30.2 16.6 %collective-permute-start.14 = (f32[2,128,128]{2,1,0:T(8,128)S(1)}, f32[2,128,128]{2,1,0:T(8,128)S(1)}, u32[]{:S(2)}, u32[]{:S(2)}) collective-permute-start(f32[2,128,128]{2,1,0:T(8,128)S(1)} %get-tuple-element.115), channel_id=1, source_target_pairs={{12,4},{13,5},{14,6},{15,7},{28,20},{29,21},{30,22},{31,23}} | collective-permute-start | bytes 393224 | tf_op jit(solution)/shard_map/ppermute | solution.py:21
  30.9 18.1 %collective-permute-start.13 = (f32[2,128,128]{2,1,0:T(8,128)S(1)}, f32[2,128,128]{2,1,0:T(8,128)S(1)}, u32[]{:S(2)}, u32[]{:S(2)}) collective-permute-start(f32[2,128,128]{2,1,0:T(8,128)S(1)} %get-tuple-element.115), channel_id=1, source_target_pairs={{8,0},{9,1},{10,2},{11,3},{24,16},{25,17},{26,18},{27,19}} | collective-permute-start | bytes 393224 | tf_op jit(solution)/shard_map/ppermute | solution.py:21
  38.7 11.6 %collective-permute-start.9 = (f32[2,128,128]{2,1,0:T(8,128)S(1)}, f32[2,128,128]{2,1,0:T(8,128)S(1)}, u32[]{:S(2)}, u32[]{:S(2)}) collective-permute-start(f32[2,128,128]{2,1,0:T(8,128)S(1)} %get-tuple-element.110.refs_0_), channel_id=1, source_target_pairs={{8,4},{9,5},{10,6},{11,7},{24,20},{25,21},{26,22},{27,23}} | collective-permute-start | bytes 393224 | tf_op jit(solution)/shard_map/ppermute | solution.py:21
  45.5 8.8 %collective-permute-start.8 = (f32[2,128,128]{2,1,0:T(8,128)S(1)}, f32[2,128,128]{2,1,0:T(8,128)S(1)}, u32[]{:S(2)}, u32[]{:S(2)}) collective-permute-start(f32[2,128,128]{2,1,0:T(8,128)S(1)} %get-tuple-element.109), channel_id=1, source_target_pairs={{8,0},{9,1},{10,2},{11,3},{24,16},{25,17},{26,18},{27,19}} | collective-permute-start | bytes 393224 | tf_op jit(solution)/shard_map/ppermute | solution.py:21
  46.8 7.5 %collective-permute-start.11 = (f32[2,128,128]{2,1,0:T(8,128)S(1)}, f32[2,128,128]{2,1,0:T(8,128)S(1)}, u32[]{:S(2)}, u32[]{:S(2)}) collective-permute-start(f32[2,128,128]{2,1,0:T(8,128)S(1)} %get-tuple-element.112), channel_id=1, source_target_pairs={{4,8},{5,9},{6,10},{7,11},{20,24},{21,25},{22,26},{23,27}} | collective-permute-start | bytes 393224 | tf_op jit(solution)/shard_map/ppermute | solution.py:21
  49.0 8.1 %collective-permute-start.10 = (f32[2,128,128]{2,1,0:T(8,128)S(1)}, f32[2,128,128]{2,1,0:T(8,128)S(1)}, u32[]{:S(2)}, u32[]{:S(2)}) collective-permute-start(f32[2,128,128]{2,1,0:T(8,128)S(1)} %shard_map.88), channel_id=1, source_target_pairs={{4,0},{5,1},{6,2},{7,3},{20,16},{21,17},{22,18},{23,19}} | collective-permute-start | bytes 393224 | tf_op jit(solution)/shard_map/ppermute | solution.py:21
  50.3 8.9 %collective-permute-start.17 = (f32[2,128,128]{2,1,0:T(8,128)S(1)}, f32[2,128,128]{2,1,0:T(8,128)S(1)}, u32[]{:S(2)}, u32[]{:S(2)}) collective-permute-start(f32[2,128,128]{2,1,0:T(8,128)S(1)} %shard_map.90.refs_1_), channel_id=1, source_target_pairs={{0,1},{1,0},{2,3},{3,2},{4,5},{5,4},{6,7},{7,6},{8,9},{9,8},{10,11... | collective-permute-start | bytes 393224 | tf_op jit(solution)/shard_map/ppermute | solution.py:596
  57.1 2.1 %collective-permute-start.16 = (f32[2,128,128]{2,1,0:T(8,128)S(1)}, f32[2,128,128]{2,1,0:T(8,128)S(1)}, u32[]{:S(2)}, u32[]{:S(2)}) collective-permute-start(f32[2,128,128]{2,1,0:T(8,128)S(1)} %shard_map.89.refs_0_), channel_id=1, source_target_pairs={{0,1},{1,0},{2,3},{3,2},{4,5},{5,4},{6,7},{7,6},{8,9},{9,8},{10,11... | collective-permute-start | bytes 393224 | tf_op jit(solution)/shard_map/ppermute | solution.py:596

commit v4 on v3

--- a/solution.py
+++ b/solution.py
@@ -185,12 +185,12 @@
     def body(cfg, kind, n, grads_at, *refs):
         here = position_of(cfg, kind)
         if kind == "all":
-            kernel(cfg, n, here, *refs)
+            kernel(cfg, kind, n, here, *refs)
             return
 
         @pl.when(here >= 0)
         def _():
-            kernel(cfg, n, here, *refs)
+            kernel(cfg, kind, n, here, *refs)
 
         @pl.when(here < 0)
         def _():
@@ -201,7 +201,20 @@
 
 
 @guarded
-def attend_kernel(cfg, n, here, *refs):
+def attend_kernel(cfg, kind, n, here, *refs):
+    if n > 4:
+        attend_rows(cfg, n, here, None, *refs)
+    elif kind == "moved":
+        attend_rows(cfg, n, here, n - 2, *refs)
+    else:
+        for far in range(n - 1):
+
+            @pl.when(jnp.maximum(here - 1, 0) == far)
+            def _():
+                attend_rows(cfg, n, here, far, *refs)
+
+
+def attend_rows(cfg, n, here, far, *refs):
     q_ref, fq_ref, a_ref, num_ref, top_ref, mass_ref, wk_t_ref, wk2_ref = refs[:8]
     kv_in = (None,) + refs[8 : 7 + n]
     win_ref, grad_ref, gden_ref, dfq_s = refs[7 + n : 11 + n]
@@ -273,8 +286,11 @@
             body(pair, 2)
             return carry
 
-        if n > 3:
-            lax.fori_loop(0, count // 2, step, 0)
+        if far is not None:
+            for first in range(0, far, 2):
+                body(first // 2, min(2, far - first))
+            return
+        lax.fori_loop(0, count // 2, step, 0)
 
         @pl.when(count % 2 == 1)
         def _():
@@ -311,6 +327,13 @@
     over_far(far_backward)
     for k in range(2, n):
         pair, at = k // 2 - 1, (k % 2) * tokens
+        if far is not None:
+            if k - 2 < far:
+                for slot in range(2):
+                    kv_out[k][slot] = dkv_s[pair, slot, at : at + tokens, :]
+            else:
+                kv_out[k][...] = jnp.zeros((2, tokens, width), F32)
+            continue
 
         @pl.when(here >= k)
         def _():
@@ -323,7 +346,7 @@
 
 
 @guarded
-def window_kernel(cfg, n, here, *refs):
+def window_kernel(cfg, kind, n, here, *refs):
     q_ref, win_ref, grad_ref, gden_ref, own_ref, prev_ref, soft_ref = refs[:7]
     outs = refs[7:]
     tokens, width = cfg.tokens, cfg.width

time: 60.6 us -> 60.4 us (level)
  no operation moved by 1% of the time
where the time goes in v4:
time: 60.4 us; the launch traced here: 60 us
  starting transfers between devices  29.3 us (49%)
  waiting for transfers between devices  19.1 us (32%)
  Pallas kernels  10.7 us (18%)
  between operations  0.94 us (2%)
    ppermute x16, starting transfers between devices, along(): return lax.ppermute(value, 'ctx', pairs)  29.2 us
    ppermute x16, waiting for transfers between devices, along(): return lax.ppermute(value, 'ctx', pairs)  19 us
    pallas_call x16, Pallas kernels, call(): pl.pallas_call(kernel, out_shape=outs, in_specs=ins or [VMEM] * len(args)...  10.7 us
  transfers between devices with their start and end apart: 18, of which 5 were waited for; matrix products, arithmetic and copies ran while one was open for 0% of the time, Pallas kernels for 14%

profile of v4, /device:TPU:0, one launch (start us, length us, event | category | flops | bytes accessed | tf_op | source)
XLA Modules:
  0.0 60.0 jit_solution(16340445053220605781)
XLA Ops:
  0.6 1.6 %shard_map.76 = (f32[2,128,128]{2,1,0:T(8,128)S(1)}, f32[2,128,128]{2,1,0:T(8,128)S(1)}, f32[128,8,128]{2,1,0:T(8,128)S(1)}, f32[8,128,128]{2,1,0:T(8,128)S(1)},...) custom-call(f32[128,4,128]{2,1,0:T(4,128)} %refs_0_.1, f32[128,4,128]{2,1,0:T(4,128)} %refs_1_.1, ...), custom_call_target="tpu_custom_call" | custom-call | tf_op jit(solution)/shard_map/pallas_call | solution.py:470
  3.6 6.2 %collective-permute-start = (f32[2,128,128]{2,1,0:T(8,128)S(1)}, f32[2,128,128]{2,1,0:T(8,128)S(1)}, u32[]{:S(2)}, u32[]{:S(2)}) collective-permute-start(f32[2,128,128]{2,1,0:T(8,128)S(1)} %get-tuple-element.64.refs_3_.refs_4_.refs_9_), channel_id=1, source_target_pairs={{0,4},{4,8},{1,5},{5,9},{2,6},{6,10},{3,7},{7,11},{16,20},{20,24},... | collective-permute-start | bytes 393224 | tf_op jit(solution)/shard_map/ppermute | solution.py:21
  9.8 3.0 %collective-permute-start.4 = (f32[2,128,128]{2,1,0:T(8,128)S(1)}, f32[2,128,128]{2,1,0:T(8,128)S(1)}, u32[]{:S(2)}, u32[]{:S(2)}) collective-permute-start(f32[2,128,128]{2,1,0:T(8,128)S(1)} %get-tuple-element.79.refs_3_.refs_4_.refs_10_), channel_id=1, source_target_pairs={{0,12},{1,13},{2,14},{3,15},{16,28},{17,29},{18,30},{19,31}} | collective-permute-start | bytes 393224 | tf_op jit(solution)/shard_map/ppermute | solution.py:21
  12.8 1.3 %collective-permute-start.3 = (f32[2,128,128]{2,1,0:T(8,128)S(1)}, f32[2,128,128]{2,1,0:T(8,128)S(1)}, u32[]{:S(2)}, u32[]{:S(2)}) collective-permute-start(f32[2,128,128]{2,1,0:T(8,128)S(1)} %get-tuple-element.79.refs_3_.refs_4_.refs_10_), channel_id=1, source_target_pairs={{0,8},{4,12},{1,9},{5,13},{2,10},{6,14},{3,11},{7,15},{16,24},{20,... | collective-permute-start | bytes 393224 | tf_op jit(solution)/shard_map/ppermute | solution.py:21
  14.1 6.8 %collective-permute-start.2 = (f32[2,128,128]{2,1,0:T(8,128)S(1)}, f32[2,128,128]{2,1,0:T(8,128)S(1)}, u32[]{:S(2)}, u32[]{:S(2)}) collective-permute-start(f32[2,128,128]{2,1,0:T(8,128)S(1)} %get-tuple-element.79.refs_3_.refs_4_.refs_10_), channel_id=1, source_target_pairs={{0,4},{4,8},{8,12},{1,5},{5,9},{9,13},{2,6},{6,10},{10,14},{3,7},{... | collective-permute-start | bytes 393224 | tf_op jit(solution)/shard_map/ppermute | solution.py:21
  20.9 1.3 %shard_map.77 = (bf16[512,384]{1,0:T(8,128)(2,1)S(1)}, bf16[4,256,256]{2,1,0:T(8,128)(2,1)S(1)}, f32[128,512]{1,0:T(8,128)S(1)}, f32[128,512]{1,0:T(8,128)S(1)},...) custom-call(f32[128,8,128]{2,1,0:T(8,128)S(1)} %get-tuple-element.61, ...), custom_call_target="tpu_custom_call" | custom-call | tf_op jit(solution)/shard_map/pallas_call | solution.py:470
  22.2 1.4 %collective-permute-start.1 = (f32[2,128,128]{2,1,0:T(8,128)S(1)}, f32[2,128,128]{2,1,0:T(8,128)S(1)}, u32[]{:S(2)}, u32[]{:S(2)}) collective-permute-start(f32[2,128,128]{2,1,0:T(8,128)S(1)} %get-tuple-element.64.refs_3_.refs_4_.refs_9_), channel_id=1, source_target_pairs={{0,8},{1,9},{2,10},{3,11},{16,24},{17,25},{18,26},{19,27}} | collective-permute-start | bytes 393224 | tf_op jit(solution)/shard_map/ppermute | solution.py:21
  24.5 1.3 %shard_map.80 = (bf16[512,384]{1,0:T(8,128)(2,1)S(1)}, bf16[4,256,256]{2,1,0:T(8,128)(2,1)S(1)}, f32[128,512]{1,0:T(8,128)S(1)}, f32[128,512]{1,0:T(8,128)S(1)},...) custom-call(f32[128,8,128]{2,1,0:T(8,128)S(1)} %get-tuple-element.61, ...), custom_call_target="tpu_custom_call" | custom-call | tf_op jit(solution)/shard_map/pallas_call | solution.py:470
  25.8 1.0 %shard_map.81 = (f32[256,512]{1,0:T(8,128)S(1)}, bf16[2,128,512]{2,1,0:T(8,128)(2,1)S(1)}, f32[1,512]{1,0:T(1,128)S(1)}, f32[4,256,128]{2,1,0:T(8,128)S(1)}, f32...) custom-call(bf16[512,384]{1,0:T(8,128)(2,1)S(1)} %get-tuple-element.80.refs_0_, ...), custom_call_target="tpu_custom_call" | custom-call | tf_op jit(solution)/shard_map/pallas_call | solution.py:470
  26.9 0.7 %shard_map.82 = (bf16[2,256,512]{2,1,0:T(8,128)(2,1)S(1)}, f32[2,128,128]{2,1,0:T(8,128)S(1)}, f32[2,128,128]{2,1,0:T(8,128)S(1)}) custom-call(bf16[512,384]{1,0:T(8,128)(2,1)S(1)} %get-tuple-element.80.refs_0_, f32[256,512]{1,0:T(8,128)S(1)} %get-tuple-element.88.refs_1_, bf16[2,128,512]{2,1,0:T(8,128)(2,1)S(1)} %get-tuple-element.89.refs_2_, ...), custom_call_target="tpu_custom_call" | custom-call | tf_op jit(solution)/shard_map/pallas_call | solution.py:470
  27.5 1.3 %collective-permute-start.12 = (f32[2,128,128]{2,1,0:T(8,128)S(1)}, f32[2,128,128]{2,1,0:T(8,128)S(1)}, u32[]{:S(2)}, u32[]{:S(2)}) collective-permute-start(f32[2,128,128]{2,1,0:T(8,128)S(1)} %get-tuple-element.114), channel_id=1, source_target_pairs={{4,0},{8,4},{12,8},{5,1},{9,5},{13,9},{6,2},{10,6},{14,10},{7,3},{... | collective-permute-start | bytes 393224 | tf_op jit(solution)/shard_map/ppermute | solution.py:21
  28.8 1.3 %collective-permute-start.15 = (f32[2,128,128]{2,1,0:T(8,128)S(1)}, f32[2,128,128]{2,1,0:T(8,128)S(1)}, u32[]{:S(2)}, u32[]{:S(2)}) collective-permute-start(f32[2,128,128]{2,1,0:T(8,128)S(1)} %get-tuple-element.116), channel_id=1, source_target_pairs={{12,0},{13,1},{14,2},{15,3},{28,16},{29,17},{30,18},{31,19}} | collective-permute-start | bytes 393224 | tf_op jit(solution)/shard_map/ppermute | solution.py:21
  30.8 1.3 %collective-permute-start.13 = (f32[2,128,128]{2,1,0:T(8,128)S(1)}, f32[2,128,128]{2,1,0:T(8,128)S(1)}, u32[]{:S(2)}, u32[]{:S(2)}) collective-permute-start(f32[2,128,128]{2,1,0:T(8,128)S(1)} %get-tuple-element.115), channel_id=1, source_target_pairs={{8,0},{9,1},{10,2},{11,3},{24,16},{25,17},{26,18},{27,19}} | collective-permute-start | bytes 393224 | tf_op jit(solution)/shard_map/ppermute | solution.py:21
  32.1 0.8 %shard_map.78 = (f32[256,512]{1,0:T(8,128)S(1)}, bf16[2,128,512]{2,1,0:T(8,128)(2,1)S(1)}, f32[1,512]{1,0:T(1,128)S(1)}, f32[4,256,128]{2,1,0:T(8,128)S(1)}, f32[2,128,128]{2,1,0:T(8,128)S(1)}) custom-call(bf16[512,384]{1,0:T(8,128)(2,1)S(1)} %get-tuple-element.65.refs_0_, bf16[4,256,256]{2,1,0:T(8,128)(2,1)S(1)} %get-tuple-element.66.refs_1_.refs_2_, ...), custom_call_target="tpu_custom_call" | custom-call | tf_op jit(solution)/shard_map/pallas_call | solution.py:470
  33.0 0.7 %shard_map.79 = (bf16[2,256,512]{2,1,0:T(8,128)(2,1)S(1)}, f32[2,128,128]{2,1,0:T(8,128)S(1)}, f32[2,128,128]{2,1,0:T(8,128)S(1)}) custom-call(bf16[512,384]{1,0:T(8,128)(2,1)S(1)} %get-tuple-element.65.refs_0_, f32[256,512]{1,0:T(8,128)S(1)} %get-tuple-element.73.refs_1_, bf16[2,128,512]{2,1,0:T(8,128)(2,1)S(1)} %get-tuple-element.74.refs_2_, ...), custom_call_target="tpu_custom_call" | custom-call | tf_op jit(solution)/shard_map/pallas_call | solution.py:470
  33.7 4.3 %collective-permute-done.12.refs_1_ = f32[2,128,128]{2,1,0:T(8,128)S(1)} collective-permute-done((f32[2,128,128]{2,1,0:T(8,128)S(1)}, f32[2,128,128]{2,1,0:T(8,128)S(1)}, u32[]{:S(2)}, u32[]{:S(2)}) %collective-permute-start.12) | collective-permute-done | bytes 131104 | tf_op jit(solution)/shard_map/ppermute | solution.py:21
  38.7 6.5 %collective-permute-done.15.refs_4_ = f32[2,128,128]{2,1,0:T(8,128)S(1)} collective-permute-done((f32[2,128,128]{2,1,0:T(8,128)S(1)}, f32[2,128,128]{2,1,0:T(8,128)S(1)}, u32[]{:S(2)}, u32[]{:S(2)}) %collective-permute-start.15) | collective-permute-done | bytes 131104 | tf_op jit(solution)/shard_map/ppermute | solution.py:21
  45.2 1.3 %collective-permute-start.8 = (f32[2,128,128]{2,1,0:T(8,128)S(1)}, f32[2,128,128]{2,1,0:T(8,128)S(1)}, u32[]{:S(2)}, u32[]{:S(2)}) collective-permute-start(f32[2,128,128]{2,1,0:T(8,128)S(1)} %get-tuple-element.109), channel_id=1, source_target_pairs={{8,0},{9,1},{10,2},{11,3},{24,16},{25,17},{26,18},{27,19}} | collective-permute-start | bytes 393224 | tf_op jit(solution)/shard_map/ppermute | solution.py:21
  47.2 1.4 %collective-permute-done.13.refs_2_ = f32[2,128,128]{2,1,0:T(8,128)S(1)} collective-permute-done((f32[2,128,128]{2,1,0:T(8,128)S(1)}, f32[2,128,128]{2,1,0:T(8,128)S(1)}, u32[]{:S(2)}, u32[]{:S(2)}) %collective-permute-start.13) | collective-permute-done | bytes 131104 | tf_op jit(solution)/shard_map/ppermute | solution.py:21
  48.7 1.3 %collective-permute-start.10 = (f32[2,128,128]{2,1,0:T(8,128)S(1)}, f32[2,128,128]{2,1,0:T(8,128)S(1)}, u32[]{:S(2)}, u32[]{:S(2)}) collective-permute-start(f32[2,128,128]{2,1,0:T(8,128)S(1)} %shard_map.88), channel_id=1, source_target_pairs={{4,0},{5,1},{6,2},{7,3},{20,16},{21,17},{22,18},{23,19}} | collective-permute-start | bytes 393224 | tf_op jit(solution)/shard_map/ppermute | solution.py:21
  50.1 3.9 %collective-permute-done.8.refs_2_ = f32[2,128,128]{2,1,0:T(8,128)S(1)} collective-permute-done((f32[2,128,128]{2,1,0:T(8,128)S(1)}, f32[2,128,128]{2,1,0:T(8,128)S(1)}, u32[]{:S(2)}, u32[]{:S(2)}) %collective-permute-start.8) | collective-permute-done | bytes 131104 | tf_op jit(solution)/shard_map/ppermute | solution.py:21
  54.0 2.8 %collective-permute-done.10.refs_4_ = f32[2,128,128]{2,1,0:T(8,128)S(1)} collective-permute-done((f32[2,128,128]{2,1,0:T(8,128)S(1)}, f32[2,128,128]{2,1,0:T(8,128)S(1)}, u32[]{:S(2)}, u32[]{:S(2)}) %collective-permute-start.10) | collective-permute-done | bytes 131104 | tf_op jit(solution)/shard_map/ppermute | solution.py:21
  57.0 2.0 %shard_map.87 = f32[128,8,128]{2,1,0:T(8,128)} custom-call(bf16[2,256,512]{2,1,0:T(8,128)(2,1)S(1)} %get-tuple-element.76.refs_0_, f32[4,256,128]{2,1,0:T(8,128)S(1)} %get-tuple-element.77.refs_1_, bf16[4,256,256]{2,1,0:T(8,128)(2,1)S(1)} %get-tuple-element.66.refs_1_.refs_2_, bf16[128,1024]{1,0:T(8,128)(2,1)S(1)} %get-tuple-element.78.refs_3_, ...), custom_call_target="tpu_custom_call" | custom-call | tf_op jit(solution)/shard_map/pallas_call | solution.py:470
  59.0 1.0 %shard_map.91 = (f32[128,4,128]{2,1,0:T(4,128)}, f32[128,4,128]{2,1,0:T(4,128)}) custom-call(f32[2,128,128]{2,1,0:T(8,128)S(1)} %shard_map.89.refs_0_, f32[2,128,128]{2,1,0:T(8,128)S(1)} %shard_map.90.refs_1_, f32[2,128,128]{2,1,0:T(8,128)S(1)} %collective-permute-done.16.refs_2_, f32[2,128,128]{2,1,0:T(8,128)S(1)} %collective-permute-done.17.refs_3_), custom_call_target="tpu_custom_call" | custom-call | tf_op jit(solution)/shard_map/pallas_call | solution.py:470
  (28 shorter events, 4.5 us)
Async XLA Ops:
  2.2 11.9 %collective-permute-start.5 = (f32[6,128,128]{2,1,0:T(8,128)S(1)}, f32[6,128,128]{2,1,0:T(8,128)S(1)}, u32[]{:S(2)}, u32[]{:S(2)}) collective-permute-start(f32[6,128,128]{2,1,0:T(8,128)S(1)} %get-tuple-element.94), channel_id=1, source_target_pairs={{12,4},{13,5},{14,6},{15,7},{28,20},{29,21},{30,22},{31,23}} | collective-permute-start | bytes 1179656 | tf_op jit(solution)/shard_map/ppermute | solution.py:21
  2.9 19.3 %collective-permute-start.6 = (f32[2,128,128]{2,1,0:T(8,128)S(1)}, f32[2,128,128]{2,1,0:T(8,128)S(1)}, u32[]{:S(2)}, u32[]{:S(2)}) collective-permute-start(f32[2,128,128]{2,1,0:T(8,128)S(1)} %get-tuple-element.64.refs_3_.refs_4_.refs_9_), channel_id=1, source_target_pairs={{8,4},{9,5},{10,6},{11,7},{24,20},{25,21},{26,22},{27,23}} | collective-permute-start | bytes 393224 | tf_op jit(solution)/shard_map/ppermute | solution.py:21
  3.6 20.1 %collective-permute-start = (f32[2,128,128]{2,1,0:T(8,128)S(1)}, f32[2,128,128]{2,1,0:T(8,128)S(1)}, u32[]{:S(2)}, u32[]{:S(2)}) collective-permute-start(f32[2,128,128]{2,1,0:T(8,128)S(1)} %get-tuple-element.64.refs_3_.refs_4_.refs_9_), channel_id=1, source_target_pairs={{0,4},{4,8},{1,5},{5,9},{2,6},{6,10},{3,7},{7,11},{16,20},{20,24},... | collective-permute-start | bytes 393224 | tf_op jit(solution)/shard_map/ppermute | solution.py:21
  9.8 16.0 %collective-permute-start.4 = (f32[2,128,128]{2,1,0:T(8,128)S(1)}, f32[2,128,128]{2,1,0:T(8,128)S(1)}, u32[]{:S(2)}, u32[]{:S(2)}) collective-permute-start(f32[2,128,128]{2,1,0:T(8,128)S(1)} %get-tuple-element.79.refs_3_.refs_4_.refs_10_), channel_id=1, source_target_pairs={{0,12},{1,13},{2,14},{3,15},{16,28},{17,29},{18,30},{19,31}} | collective-permute-start | bytes 393224 | tf_op jit(solution)/shard_map/ppermute | solution.py:21
  12.8 13.0 %collective-permute-start.3 = (f32[2,128,128]{2,1,0:T(8,128)S(1)}, f32[2,128,128]{2,1,0:T(8,128)S(1)}, u32[]{:S(2)}, u32[]{:S(2)}) collective-permute-start(f32[2,128,128]{2,1,0:T(8,128)S(1)} %get-tuple-element.79.refs_3_.refs_4_.refs_10_), channel_id=1, source_target_pairs={{0,8},{4,12},{1,9},{5,13},{2,10},{6,14},{3,11},{7,15},{16,24},{20,... | collective-permute-start | bytes 393224 | tf_op jit(solution)/shard_map/ppermute | solution.py:21
  14.1 11.7 %collective-permute-start.2 = (f32[2,128,128]{2,1,0:T(8,128)S(1)}, f32[2,128,128]{2,1,0:T(8,128)S(1)}, u32[]{:S(2)}, u32[]{:S(2)}) collective-permute-start(f32[2,128,128]{2,1,0:T(8,128)S(1)} %get-tuple-element.79.refs_3_.refs_4_.refs_10_), channel_id=1, source_target_pairs={{0,4},{4,8},{8,12},{1,5},{5,9},{9,13},{2,6},{6,10},{10,14},{3,7},{... | collective-permute-start | bytes 393224 | tf_op jit(solution)/shard_map/ppermute | solution.py:21
  22.2 8.6 %collective-permute-start.1 = (f32[2,128,128]{2,1,0:T(8,128)S(1)}, f32[2,128,128]{2,1,0:T(8,128)S(1)}, u32[]{:S(2)}, u32[]{:S(2)}) collective-permute-start(f32[2,128,128]{2,1,0:T(8,128)S(1)} %get-tuple-element.64.refs_3_.refs_4_.refs_9_), channel_id=1, source_target_pairs={{0,8},{1,9},{2,10},{3,11},{16,24},{17,25},{18,26},{19,27}} | collective-permute-start | bytes 393224 | tf_op jit(solution)/shard_map/ppermute | solution.py:21
  23.8 33.0 %collective-permute-start.7 = (f32[6,128,128]{2,1,0:T(8,128)S(1)}, f32[6,128,128]{2,1,0:T(8,128)S(1)}, u32[]{:S(2)}, u32[]{:S(2)}) collective-permute-start(f32[6,128,128]{2,1,0:T(8,128)S(1)} %shard_map.86), channel_id=1, source_target_pairs={{4,12},{5,13},{6,14},{7,15},{20,28},{21,29},{22,30},{23,31}} | collective-permute-start | bytes 1179656 | tf_op jit(solution)/shard_map/ppermute | solution.py:21
  27.5 10.5 %collective-permute-start.12 = (f32[2,128,128]{2,1,0:T(8,128)S(1)}, f32[2,128,128]{2,1,0:T(8,128)S(1)}, u32[]{:S(2)}, u32[]{:S(2)}) collective-permute-start(f32[2,128,128]{2,1,0:T(8,128)S(1)} %get-tuple-element.114), channel_id=1, source_target_pairs={{4,0},{8,4},{12,8},{5,1},{9,5},{13,9},{6,2},{10,6},{14,10},{7,3},{... | collective-permute-start | bytes 393224 | tf_op jit(solution)/shard_map/ppermute | solution.py:21
  28.8 16.4 %collective-permute-start.15 = (f32[2,128,128]{2,1,0:T(8,128)S(1)}, f32[2,128,128]{2,1,0:T(8,128)S(1)}, u32[]{:S(2)}, u32[]{:S(2)}) collective-permute-start(f32[2,128,128]{2,1,0:T(8,128)S(1)} %get-tuple-element.116), channel_id=1, source_target_pairs={{12,0},{13,1},{14,2},{15,3},{28,16},{29,17},{30,18},{31,19}} | collective-permute-start | bytes 393224 | tf_op jit(solution)/shard_map/ppermute | solution.py:21
  30.1 16.4 %collective-permute-start.14 = (f32[2,128,128]{2,1,0:T(8,128)S(1)}, f32[2,128,128]{2,1,0:T(8,128)S(1)}, u32[]{:S(2)}, u32[]{:S(2)}) collective-permute-start(f32[2,128,128]{2,1,0:T(8,128)S(1)} %get-tuple-element.115), channel_id=1, source_target_pairs={{12,4},{13,5},{14,6},{15,7},{28,20},{29,21},{30,22},{31,23}} | collective-permute-start | bytes 393224 | tf_op jit(solution)/shard_map/ppermute | solution.py:21
  30.8 17.8 %collective-permute-start.13 = (f32[2,128,128]{2,1,0:T(8,128)S(1)}, f32[2,128,128]{2,1,0:T(8,128)S(1)}, u32[]{:S(2)}, u32[]{:S(2)}) collective-permute-start(f32[2,128,128]{2,1,0:T(8,128)S(1)} %get-tuple-element.115), channel_id=1, source_target_pairs={{8,0},{9,1},{10,2},{11,3},{24,16},{25,17},{26,18},{27,19}} | collective-permute-start | bytes 393224 | tf_op jit(solution)/shard_map/ppermute | solution.py:21
  38.0 12.0 %collective-permute-start.9 = (f32[2,128,128]{2,1,0:T(8,128)S(1)}, f32[2,128,128]{2,1,0:T(8,128)S(1)}, u32[]{:S(2)}, u32[]{:S(2)}) collective-permute-start(f32[2,128,128]{2,1,0:T(8,128)S(1)} %get-tuple-element.110.refs_0_), channel_id=1, source_target_pairs={{8,4},{9,5},{10,6},{11,7},{24,20},{25,21},{26,22},{27,23}} | collective-permute-start | bytes 393224 | tf_op jit(solution)/shard_map/ppermute | solution.py:21
  45.2 8.8 %collective-permute-start.8 = (f32[2,128,128]{2,1,0:T(8,128)S(1)}, f32[2,128,128]{2,1,0:T(8,128)S(1)}, u32[]{:S(2)}, u32[]{:S(2)}) collective-permute-start(f32[2,128,128]{2,1,0:T(8,128)S(1)} %get-tuple-element.109), channel_id=1, source_target_pairs={{8,0},{9,1},{10,2},{11,3},{24,16},{25,17},{26,18},{27,19}} | collective-permute-start | bytes 393224 | tf_op jit(solution)/shard_map/ppermute | solution.py:21
  46.5 7.5 %collective-permute-start.11 = (f32[2,128,128]{2,1,0:T(8,128)S(1)}, f32[2,128,128]{2,1,0:T(8,128)S(1)}, u32[]{:S(2)}, u32[]{:S(2)}) collective-permute-start(f32[2,128,128]{2,1,0:T(8,128)S(1)} %get-tuple-element.112), channel_id=1, source_target_pairs={{4,8},{5,9},{6,10},{7,11},{20,24},{21,25},{22,26},{23,27}} | collective-permute-start | bytes 393224 | tf_op jit(solution)/shard_map/ppermute | solution.py:21
  48.7 8.1 %collective-permute-start.10 = (f32[2,128,128]{2,1,0:T(8,128)S(1)}, f32[2,128,128]{2,1,0:T(8,128)S(1)}, u32[]{:S(2)}, u32[]{:S(2)}) collective-permute-start(f32[2,128,128]{2,1,0:T(8,128)S(1)} %shard_map.88), channel_id=1, source_target_pairs={{4,0},{5,1},{6,2},{7,3},{20,16},{21,17},{22,18},{23,19}} | collective-permute-start | bytes 393224 | tf_op jit(solution)/shard_map/ppermute | solution.py:21
  50.0 9.0 %collective-permute-start.17 = (f32[2,128,128]{2,1,0:T(8,128)S(1)}, f32[2,128,128]{2,1,0:T(8,128)S(1)}, u32[]{:S(2)}, u32[]{:S(2)}) collective-permute-start(f32[2,128,128]{2,1,0:T(8,128)S(1)} %shard_map.90.refs_1_), channel_id=1, source_target_pairs={{0,1},{1,0},{2,3},{3,2},{4,5},{5,4},{6,7},{7,6},{8,9},{9,8},{10,11... | collective-permute-start | bytes 393224 | tf_op jit(solution)/shard_map/ppermute | solution.py:619
  56.9 2.1 %collective-permute-start.16 = (f32[2,128,128]{2,1,0:T(8,128)S(1)}, f32[2,128,128]{2,1,0:T(8,128)S(1)}, u32[]{:S(2)}, u32[]{:S(2)}) collective-permute-start(f32[2,128,128]{2,1,0:T(8,128)S(1)} %shard_map.89.refs_0_), channel_id=1, source_target_pairs={{0,1},{1,0},{2,3},{3,2},{4,5},{5,4},{6,7},{7,6},{8,9},{9,8},{10,11... | collective-permute-start | bytes 393224 | tf_op jit(solution)/shard_map/ppermute | solution.py:619
